TPU v7x, 512 devices: a whole 4x4x16 slice. The times are simulated.
512 devices in a mesh: head: 16 (over y, x), tok: 32 (over z, core).
Axes of the slice: x: 4, y: 4, z: 16, core: 2. Of those that a mesh axis runs over, the one named last changes fastest.
Arguments:
- stretch_tokens: bfloat16 [32, 1024, 1792], P('tok', 'head'), may hold values from -6 to 6
- stretch_tail: bfloat16 [32, 2, 1792], P('tok'), may hold values from -6 to 6
- decode_tokens: bfloat16 [32, 32, 1792], P('tok'), may hold values from -6 to 6
- decode_tail: bfloat16 [32, 32, 2, 1792], P('tok'), may hold values from -6 to 6
- norm_gain: float32 [1792], replicated, may hold values from 0.1 to 1.9
- conv_taps: float32 [3, 1792], replicated, may hold values from -3 to 3
- qkv_weight: bfloat16 [1792, 16, 144], P(None, 'head'), may hold values from -0.125 to 0.125
- out_gain: float32 [1792], P('head'), may hold values from 0.1 to 1.9
- out_weight: bfloat16 [1792, 1792], P('head'), may hold values from -0.125 to 0.125
- state_cache: float32 [32, 16, 16, 112, 273], P('tok', None, 'head'), may hold values from -24 to 24
- stretch_len: int32 [32], P('tok'), may hold values from 1 to 1024, 16384 in all
- stretch_slot: int32 [32], P('tok'), may hold values from 0 to 15
- decode_slot: int32 [32, 32], P('tok'), may hold values from 0 to 15
- decode_owner: int32 [32, 32, 1], P('tok'), may hold values from 0 to 31; in each aligned block of 32 rows (0 to 31, 32 to 63, ..., all dimensions but the last counted through in order) at most 2 rows name the same one
Outputs:
- stretch_out: bfloat16 [32, 1024, 1792], P('tok', 'head')
- decode_out: bfloat16 [32, 32, 1792], P('tok', 'head')
- state_new: float32 [32, 16, 112, 273], P('tok', 'head')
Inputs may be any that keep to these rules, and one draw needn't show every extreme that they name: `decode_owner`: in the 32 decoders of one group at most 2 name the same owner group, a bound that some block reaches of them. `stretch_len`: some group's stretch is full.
All inputs are finite; a program needn't handle non-finite values.
Results may differ from a plain program's by a relative error of at most 0.014.
Values may be sent and summed in bfloat16 or wider, within the bound.
A program may use at most 64 MiB of HBM per device.

v0:
```python
import math

import jax
import jax.numpy as jnp
from jax import lax
from jax.sharding import PartitionSpec as P

D = 1792
DH = 112
F = 16
STRETCH = 1024
DEC = 32


def from_behind(array, axis, by):
    peers = lax.axis_size(axis)
    pairs = [(i, i + by) for i in range(peers) if 0 <= i + by < peers]
    return lax.ppermute(array, axis, pairs)


def rms_rows(values, gain):
    values = values.astype(jnp.float32)
    factor = lax.rsqrt(jnp.mean(values * values, axis=-1, keepdims=True) + 1e-05)
    return values * factor * gain


def features(vectors):
    breadth = vectors.shape[-1]
    linear = vectors / math.sqrt(math.sqrt(breadth))
    outer = vectors[..., :, None] * vectors[..., None, :] / math.sqrt(2.0 * breadth)
    outer = outer.reshape(vectors.shape[:-1] + (breadth * breadth,))
    ones = jnp.ones(vectors.shape[:-1] + (1,), vectors.dtype)
    return jnp.concatenate([ones, linear, outer], axis=-1)


def convolve(tail, normed, conv_taps):
    joined = jnp.concatenate([tail, normed], axis=-2).astype(jnp.float32)
    span_rows = normed.shape[-2]
    total = conv_taps[0] * joined[..., 0:span_rows, :]
    total = total + conv_taps[1] * joined[..., 1 : span_rows + 1, :]
    total = total + conv_taps[2] * joined[..., 2 : span_rows + 2, :]
    return total.astype(jnp.bfloat16)


def decode_items(items, slot_items, cache_own, out_gain, head_count):
    item_count = items.shape[0]
    shaped = items.reshape(item_count, head_count, 2 * F + DH).astype(jnp.float32)
    queries = shaped[:, :, :F]
    key_feats = shaped[:, :, F : 2 * F]
    values = shaped[:, :, 2 * F :]
    slot_total = cache_own.shape[0]
    table = jnp.einsum(
        "nhp,shdp->nshd", features(queries), cache_own, precision=lax.Precision.HIGHEST
    )
    picker = (slot_items[:, None] == jnp.arange(slot_total)[None, :]).astype(jnp.float32)
    carried = jnp.einsum("ns,nshd->nhd", picker, table, precision=lax.Precision.HIGHEST)
    inner = jnp.sum(queries * key_feats, axis=-1) / math.sqrt(F)
    own_term = (1.0 + inner + 0.5 * inner * inner)[..., None] * values
    attended = rms_rows(carried + own_term, out_gain.reshape(head_count, DH))
    return attended.astype(jnp.bfloat16).reshape(item_count, head_count * DH)


def local(
    stretch_tokens,
    stretch_tail,
    decode_tokens,
    decode_tail,
    norm_gain,
    conv_taps,
    qkv_weight,
    out_gain,
    out_weight,
    state_cache,
    stretch_len,
    stretch_slot,
    decode_slot,
    decode_owner,
):
    head_count = qkv_weight.shape[1]
    block_width = qkv_weight.shape[2]
    rows_own = stretch_tokens.shape[1]
    w_flat = qkv_weight.reshape(D, head_count * block_width)
    gains = out_gain.reshape(head_count, DH)
    normed = rms_rows(stretch_tokens[0], norm_gain).astype(jnp.bfloat16)
    rim_rows = from_behind(normed[rows_own - 2 :], "head", 1)
    first_dev = lax.axis_index("head") == 0
    rim_rows = jnp.where(first_dev, stretch_tail[0], rim_rows)
    conved = convolve(rim_rows, normed, conv_taps)
    grouped = jnp.dot(
        lax.all_gather(conved, "head", axis=0, tiled=True),
        w_flat,
        preferred_element_type=jnp.float32,
    ).astype(jnp.bfloat16)
    grouped = grouped.reshape(STRETCH, head_count, block_width)
    queries = grouped[:, :, :F]
    key_feats = grouped[:, :, F : 2 * F]
    values = grouped[:, :, 2 * F :]
    length = stretch_len[0]
    positions = jnp.arange(STRETCH)
    valid_rows = positions < length
    state_old = lax.dynamic_index_in_dim(state_cache[0], stretch_slot[0], 0, keepdims=False)
    carried = jnp.einsum(
        "ihp,hdp->ihd",
        features(queries.astype(jnp.float32)),
        state_old,
        precision=lax.Precision.HIGHEST,
    )
    block_rows = min(512, STRETCH)
    pieces = []
    for anchor in range(0, STRETCH, block_rows):
        finish = anchor + block_rows
        inner = jnp.einsum(
            "ihf,jhf->hij",
            queries[anchor:finish],
            key_feats[:finish],
            preferred_element_type=jnp.float32,
        ) / math.sqrt(F)
        weights = 1.0 + inner + 0.5 * inner * inner
        allowed = (positions[None, :finish] <= positions[anchor:finish, None]) & valid_rows[
            None, :finish
        ]
        weights = jnp.where(allowed[None], weights, 0.0).astype(jnp.bfloat16)
        pieces.append(
            jnp.einsum("hij,jhd->ihd", weights, values[:finish], preferred_element_type=jnp.float32)
        )
    local_sum = jnp.concatenate(pieces, axis=0)
    attended = rms_rows(carried + local_sum, gains)
    attended = (
        jnp.where(valid_rows[:, None, None], attended, 0.0)
        .astype(jnp.bfloat16)
        .reshape(STRETCH, head_count * DH)
    )
    key_phi = jnp.where(
        valid_rows[:, None, None], features(key_feats.astype(jnp.float32)), 0.0
    ).astype(jnp.bfloat16)
    state_next = state_old + jnp.einsum(
        "jhd,jhp->hdp", values, key_phi, preferred_element_type=jnp.float32
    )
    part_rows = attended
    stretch_out = lax.psum_scatter(
        jnp.dot(part_rows, out_weight, preferred_element_type=jnp.float32).astype(jnp.bfloat16),
        "head",
        scatter_dimension=0,
        tiled=True,
    )
    dec_normed = rms_rows(decode_tokens[0], norm_gain).astype(jnp.bfloat16)
    dec_conved = convolve(decode_tail[0], dec_normed[:, None, :], conv_taps)[:, 0, :]
    dec_qkv = jnp.dot(dec_conved, w_flat, preferred_element_type=jnp.float32).astype(jnp.bfloat16)
    owners = decode_owner[0, :, 0]
    slots_here = decode_slot[0]
    groups = lax.axis_size("tok")
    capacity = max(2, 2 * DEC // groups)
    earlier = jnp.arange(DEC)[None, :] < jnp.arange(DEC)[:, None]
    same_owner = owners[None, :] == owners[:, None]
    rank_in = jnp.sum(earlier & same_owner, axis=1)
    target = owners * capacity + rank_in
    placing = jnp.arange(groups * capacity)[:, None] == target[None, :]
    sent_rows = jnp.dot(
        placing.astype(jnp.bfloat16), dec_qkv, preferred_element_type=jnp.float32
    ).astype(jnp.bfloat16)
    sent_rows = sent_rows.reshape(groups, capacity, head_count * block_width)
    sent_slots = jnp.sum(jnp.where(placing, slots_here[None, :] + 1, 0), axis=1) - 1
    sent_slots = sent_slots.reshape(groups, capacity)
    item_rows = lax.all_to_all(sent_rows, "tok", split_axis=0, concat_axis=0, tiled=True)
    item_slots = lax.all_to_all(sent_slots, "tok", split_axis=0, concat_axis=0, tiled=True)
    item_count = item_rows.shape[1]
    flat_out = decode_items(
        item_rows.reshape(groups * item_count, head_count * block_width),
        item_slots.reshape(groups * item_count),
        state_cache[0],
        out_gain,
        head_count,
    )
    served = flat_out.reshape(groups, item_count, head_count * DH)
    returned = lax.all_to_all(served, "tok", split_axis=0, concat_axis=0, tiled=True)
    dec_attended = jnp.dot(
        jnp.transpose(placing).astype(jnp.bfloat16),
        returned.reshape(groups * capacity, head_count * DH),
        preferred_element_type=jnp.float32,
    ).astype(jnp.bfloat16)
    part_rows = dec_attended
    decode_out = lax.psum_scatter(
        jnp.dot(part_rows, out_weight, preferred_element_type=jnp.float32).astype(jnp.bfloat16),
        "head",
        scatter_dimension=0,
        tiled=True,
    )
    return (stretch_out[None], decode_out[None], state_next[None])


def solution(mesh):
    in_specs = (
        P("tok", "head", None),
        P("tok", None, None),
        P("tok", None, None),
        P("tok", None, None, None),
        P(),
        P(),
        P(None, "head", None),
        P("head"),
        P("head", None),
        P("tok", None, "head", None, None),
        P("tok"),
        P("tok"),
        P("tok", None),
        P("tok", None, None),
    )
    out_specs = (P("tok", "head", None), P("tok", "head", None), P("tok", "head", None, None))
    return jax.shard_map(local, mesh=mesh, in_specs=in_specs, out_specs=out_specs, check_vma=False)
```

profile of v0, /device:TPU:1, one launch (start us, length us, event | category | flops | bytes accessed | tf_op | source)
XLA Modules:
  0.0 305.1 jit_solution(336540737238835392)
XLA Ops:
  7.3 1.2 fusion.37
  8.5 1.1 fusion.39
  9.6 3.9 %collective-permute-start = (bf16[2,1792]{1,0:T(2,128)(2,1)S(1)}, bf16[2,1792]{1,0:T(2,128)(2,1)S(1)}, u32[]{:S(2)}, u32[]{:S(2)}) collective-permute-start(bf16[2,1792]{1,0:T(2,128)(2,1)S(1)} %slice.100), channel_id=1, source_target_pairs={{0,32},{32,64},{64,96},{96,128},{128,160},{160,192},{192,224},{224... | collective-permute-start | bytes 21512 | tf_op jit(solution)/shard_map/ppermute | solution.py:18
  13.6 0.9 slice_reduce_fusion.2
  14.5 0.7 broadcast_select_fusion
  15.3 0.8 fusion.41
  16.5 0.7 sub.7
  17.2 16.6 %all-to-all-start = ((s32[32,1,2]{2,1,0:T(1,128)}), s32[32,1,2]{2,1,0:T(1,128)S(1)}, u32[]{:S(2)}, u32[]{:S(2)}) async-start(s32[32,1,2]{2,1,0:T(1,128)} %bitcast.26), calls=%async_computation.1 | async-start | bytes 32768 | tf_op jit(solution)/shard_map/all_to_all | solution.py:165
  34.8 0.9 maximum_convert_fusion
  35.7 1.6 convolution_convert_fusion.3
  37.9 0.6 reshape.492
  38.6 7.0 %all-to-all-done = s32[32,1,2]{2,1,0:T(1,128)S(1)} async-done(((s32[32,1,2]{2,1,0:T(1,128)}), s32[32,1,2]{2,1,0:T(1,128)S(1)}, u32[]{:S(2)}, u32[]{:S(2)}) %all-to-all-start) | async-done | bytes 288 | tf_op jit(solution)/shard_map/all_to_all | solution.py:165
  45.6 5.1 %all-to-all-start.1 = ((bf16[32,2,144]{2,1,0:T(2,128)(2,1)}), bf16[32,2,144]{2,1,0:T(2,128)(2,1)S(1)}, u32[]{:S(2)}, u32[]{:S(2)}) async-start(bf16[32,2,144]{2,1,0:T(2,128)(2,1)} %reshape.492), calls=%async_computation.2 | async-start | bytes 65536 | tf_op jit(solution)/shard_map/all_to_all | solution.py:164
  52.1 10.7 %all-to-all-done.1 = bf16[32,2,144]{2,1,0:T(2,128)(2,1)S(1)} async-done(((bf16[32,2,144]{2,1,0:T(2,128)(2,1)}), bf16[32,2,144]{2,1,0:T(2,128)(2,1)S(1)}, u32[]{:S(2)}, u32[]{:S(2)}) %all-to-all-start.1) | async-done | bytes 18464 | tf_op jit(solution)/shard_map/all_to_all | solution.py:164
  62.9 0.7 fusion.74
  63.7 0.7 copy.50
  65.0 2.6 fusion
  67.6 0.7 fusion.25
  68.5 0.7 multiply_convert_fusion
  69.2 4.6 %all-to-all-start.2 = ((bf16[32,2,112]{2,1,0:T(2,128)(2,1)}), bf16[32,2,112]{2,1,0:T(2,128)(2,1)S(1)}, u32[]{:S(2)}, u32[]{:S(2)}) async-start(bf16[32,2,112]{2,1,0:T(2,128)(2,1)} %bitcast.40), calls=%async_computation.3 | async-start | bytes 32768 | tf_op jit(solution)/shard_map/all_to_all | solution.py:175
  74.0 11.7 %all-to-all-done.2 = bf16[32,2,112]{2,1,0:T(2,128)(2,1)S(1)} async-done(((bf16[32,2,112]{2,1,0:T(2,128)(2,1)}), bf16[32,2,112]{2,1,0:T(2,128)(2,1)S(1)}, u32[]{:S(2)}, u32[]{:S(2)}) %all-to-all-start.2) | async-done | bytes 14368 | tf_op jit(solution)/shard_map/all_to_all | solution.py:175
  85.7 1.0 convolution_convert_fusion.1
  86.8 3.4 %fusion.6 = bf16[1024,1,144]{0,2,1:T(8,128)(2,1)S(1)} fusion(bf16[1024,1792]{1,0:T(8,128)(2,1)} %all-gather.2.cloned.1.call-done, bf16[1792,1,144]{0,2,1:T(8,128)(2,1)S(1)} %copy-done), kind=kOutput, calls=%fused_computation.12 | convolution fusion | flops 528629760 | bytes 4481024 | tf_op jit(solution)/shard_map/dot_general | solution.py:89
  90.3 1.1 fusion.7
  91.5 0.7 convolution_bitcast_fusion.1
  92.2 1.2 multiply_reduce_fusion
  93.4 3.0 convolution_convert_fusion
  96.5 1.3 dynamic-slice.1
  98.4 103.7 %all-reduce.3.cloned.1.call-done = bf16[32,1792]{1,0:T(8,128)(2,1)} async-done(((bf16[32,1792]{1,0:T(8,128)(2,1)}), bf16[32,1792]{1,0:T(8,128)(2,1)}) %all-reduce.3.cloned.1.call-update) | async-done | bytes 114704
  202.1 1.4 dynamic-slice_bitcast_fusion
  204.0 0.8 copy.53
  204.8 93.8 %reduce-scatter.2.cloned.1.call-done = bf16[64,1792]{1,0:T(8,128)(2,1)} async-done(((bf16[1024,1792]{1,0:T(8,128)(2,1)}), bf16[64,1792]{1,0:T(8,128)(2,1)}) %reduce-scatter.2.cloned.1.call-update) | async-done | bytes 229392 | tf_op jit(solution)/shard_map/reduce_scatter | solution.py:140
  (69 shorter events, 3.8 us)
Async XLA Ops:
  7.2 28.5 %copy-start = (bf16[1792,1,144]{0,2,1:T(8,128)(2,1)S(1)}, bf16[1792,1,144]{0,2,1:T(8,128)(2,1)}, u32[]{:S(2)}) copy-start(bf16[1792,1,144]{0,2,1:T(8,128)(2,1)} %param.20) | copy-start | bytes 1548292
  7.2 27.5 %copy-start.7 = (f32[1792]{0:T(1024)S(1)}, f32[1792]{0:T(1024)}, u32[]{:S(2)}) copy-start(f32[1792]{0:T(1024)} %param.18) | copy-start | bytes 21508
  7.2 9.0 %copy-start.11 = (s32[1,32,1]{1,2,0:T(1,128)S(1)}, s32[1,32,1]{1,2,0:T(1,128)}, u32[]{:S(2)}) copy-start(s32[1,32,1]{1,2,0:T(1,128)} %param.27) | copy-start | bytes 388
  7.2 9.1 %copy-start.10 = (s32[1,32]{1,0:T(1,128)S(1)}, s32[1,32]{1,0:T(1,128)}, u32[]{:S(2)}) copy-start(s32[1,32]{1,0:T(1,128)} %param.26) | copy-start | bytes 388
  7.2 27.2 %copy-start.4 = (bf16[1,32,2,1792]{3,2,1,0:T(2,128)(2,1)S(1)}, bf16[1,32,2,1792]{3,2,1,0:T(2,128)(2,1)}, u32[]{:S(2)}) copy-start(bf16[1,32,2,1792]{3,2,1,0:T(2,128)(2,1)} %param.17) | copy-start | bytes 688132
  7.2 27.3 %copy-start.3 = (bf16[1,32,1792]{2,1,0:T(8,128)(2,1)S(1)}, bf16[1,32,1792]{2,1,0:T(8,128)(2,1)}, u32[]{:S(2)}) copy-start(bf16[1,32,1792]{2,1,0:T(8,128)(2,1)} %param.16) | copy-start | bytes 344068
  7.2 79.6 %all-gather.2.cloned.1.call-start = ((), (), s32[]{:S(2)}) async-start(), calls=%async_computation.4 | async-start | bytes 3899392 | tf_op jit(solution)/shard_map/all_gather | solution.py:90
  9.6 4.9 %collective-permute-start = (bf16[2,1792]{1,0:T(2,128)(2,1)S(1)}, bf16[2,1792]{1,0:T(2,128)(2,1)S(1)}, u32[]{:S(2)}, u32[]{:S(2)}) collective-permute-start(bf16[2,1792]{1,0:T(2,128)(2,1)S(1)} %slice.100), channel_id=1, source_target_pairs={{0,32},{32,64},{64,96},{96,128},{128,160},{160,192},{192,224},{224... | collective-permute-start | bytes 21512 | tf_op jit(solution)/shard_map/ppermute | solution.py:18
  15.3 22.0 %copy-start.1 = (f32[1,16,1,112,273]{3,2,4,1,0:T(1,128)S(1)}, f32[1,16,1,112,273]{3,2,4,1,0:T(1,128)}, u32[]{:S(2)}) copy-start(f32[1,16,1,112,273]{3,2,4,1,0:T(1,128)} %param.23) | copy-start | bytes 5870596
  17.2 28.4 %all-to-all-start = ((s32[32,1,2]{2,1,0:T(1,128)}), s32[32,1,2]{2,1,0:T(1,128)S(1)}, u32[]{:S(2)}, u32[]{:S(2)}) async-start(s32[32,1,2]{2,1,0:T(1,128)} %bitcast.26), calls=%async_computation.1 | async-start | bytes 32768 | tf_op jit(solution)/shard_map/all_to_all | solution.py:165
  45.6 17.2 %all-to-all-start.1 = ((bf16[32,2,144]{2,1,0:T(2,128)(2,1)}), bf16[32,2,144]{2,1,0:T(2,128)(2,1)S(1)}, u32[]{:S(2)}, u32[]{:S(2)}) async-start(bf16[32,2,144]{2,1,0:T(2,128)(2,1)} %reshape.492), calls=%async_computation.2 | async-start | bytes 65536 | tf_op jit(solution)/shard_map/all_to_all | solution.py:164
  52.1 16.4 %copy-start.9 = (f32[112]{0:T(128)S(1)}, f32[112]{0:T(128)}, u32[]{:S(2)}) copy-start(f32[112]{0:T(128)} %param.21) | copy-start | bytes 1348
  62.9 22.8 %copy-start.2 = (bf16[112,1792]{1,0:T(8,128)(2,1)S(1)}, bf16[112,1792]{1,0:T(8,128)(2,1)}, u32[]{:S(2)}) copy-start(bf16[112,1792]{1,0:T(8,128)(2,1)} %param.22) | copy-start | bytes 1204228
  69.2 16.5 %all-to-all-start.2 = ((bf16[32,2,112]{2,1,0:T(2,128)(2,1)}), bf16[32,2,112]{2,1,0:T(2,128)(2,1)S(1)}, u32[]{:S(2)}, u32[]{:S(2)}) async-start(bf16[32,2,112]{2,1,0:T(2,128)(2,1)} %bitcast.40), calls=%async_computation.3 | async-start | bytes 32768 | tf_op jit(solution)/shard_map/all_to_all | solution.py:175
  73.9 128.2 %all-reduce.3.cloned.1.call-start = ((), (), s32[]{:S(2)}) async-start(), calls=%async_computation.6 | async-start | bytes 229376
  74.0 16.2 %copy-start.8 = (s32[1024]{0:T(1024)}, s32[1024]{0:T(1024)S(1)}, u32[]{:S(2)}) copy-start(s32[1024]{0:T(1024)S(1)} %iota.31) | copy-start | bytes 12292
  86.7 211.9 %reduce-scatter.2.cloned.1.call-start = ((), (), s32[]{:S(2)}) async-start(), calls=%async_computation.5 | async-start | bytes 3899392 | tf_op jit(solution)/shard_map/reduce_scatter | solution.py:140
  90.2 1.3 copy-start.5
  90.2 1.2 slice-start
  96.4 107.1 %copy-start.6 = (bf16[1024,1,144]{0,2,1:T(8,128)(2,1)S(1)}, bf16[1024,1,144]{0,2,1:T(8,128)(2,1)}, u32[]{:S(2)}) copy-start(bf16[1024,1,144]{0,2,1:T(8,128)(2,1)} %copy-done.5) | copy-start | bytes 884740
Sparse Core Ops, SparseCore 0:
  16.3 70.3 all-gather.1
  90.4 111.5 all-reduce.2
  206.9 91.6 reduce-scatter.1
where the time goes:
time: 306 us; the launch traced here: 305 us
  waiting for transfers between devices  227 us (74%)
  starting transfers between devices  30.4 us (10%)
  between operations  16.2 us (5%)
  matrix products  15.7 us (5%)
  other arithmetic  8.49 us (3%)
  local copies, waits for them, and re-layouts  7.29 us (2%)
    unnamed x4, waiting for transfers between devices  104 us
    reduce_scatter x1, waiting for transfers between devices, local(): lax.psum_scatter(jnp.dot(part_rows, out_weight, preferred_element_type=jn...  93.8 us
    all_to_all x1, starting transfers between devices, local(): lax.all_to_all(sent_slots, 'tok', split_axis=0, concat_axis=0, tiled=True)  16.6 us
    all_to_all x1, waiting for transfers between devices, local(): lax.all_to_all(served, 'tok', split_axis=0, concat_axis=0, tiled=True)  11.7 us
    all_to_all x1, waiting for transfers between devices, local(): lax.all_to_all(sent_rows, 'tok', split_axis=0, concat_axis=0, tiled=True)  10.7 us
    all_to_all x1, waiting for transfers between devices, local(): lax.all_to_all(sent_slots, 'tok', split_axis=0, concat_axis=0, tiled=True)  7.05 us
  transfers between devices with their start and end apart: 7, of which 5 were waited for; matrix products, arithmetic and copies ran while one was open for 9% of the time, Pallas kernels for 0%

commit v1 on v0

--- a/solution.py
+++ b/solution.py
@@ -136,13 +136,7 @@
     state_next = state_old + jnp.einsum(
         "jhd,jhp->hdp", values, key_phi, preferred_element_type=jnp.float32
     )
-    part_rows = attended
-    stretch_out = lax.psum_scatter(
-        jnp.dot(part_rows, out_weight, preferred_element_type=jnp.float32).astype(jnp.bfloat16),
-        "head",
-        scatter_dimension=0,
-        tiled=True,
-    )
+    stretch_part = jnp.dot(attended, out_weight, preferred_element_type=jnp.float32).astype(jnp.bfloat16)
     dec_normed = rms_rows(decode_tokens[0], norm_gain).astype(jnp.bfloat16)
     dec_conved = convolve(decode_tail[0], dec_normed[:, None, :], conv_taps)[:, 0, :]
     dec_qkv = jnp.dot(dec_conved, w_flat, preferred_element_type=jnp.float32).astype(jnp.bfloat16)
@@ -160,9 +154,11 @@
     ).astype(jnp.bfloat16)
     sent_rows = sent_rows.reshape(groups, capacity, head_count * block_width)
     sent_slots = jnp.sum(jnp.where(placing, slots_here[None, :] + 1, 0), axis=1) - 1
-    sent_slots = sent_slots.reshape(groups, capacity)
+    sent_slots = sent_slots.reshape(groups, capacity, 1).astype(jnp.bfloat16)
+    sent_rows = jnp.concatenate([sent_rows, sent_slots], axis=2)
     item_rows = lax.all_to_all(sent_rows, "tok", split_axis=0, concat_axis=0, tiled=True)
-    item_slots = lax.all_to_all(sent_slots, "tok", split_axis=0, concat_axis=0, tiled=True)
+    item_slots = item_rows[:, :, -1].astype(jnp.int32)
+    item_rows = item_rows[:, :, :-1]
     item_count = item_rows.shape[1]
     flat_out = decode_items(
         item_rows.reshape(groups * item_count, head_count * block_width),
@@ -178,13 +174,17 @@
         returned.reshape(groups * capacity, head_count * DH),
         preferred_element_type=jnp.float32,
     ).astype(jnp.bfloat16)
-    part_rows = dec_attended
-    decode_out = lax.psum_scatter(
-        jnp.dot(part_rows, out_weight, preferred_element_type=jnp.float32).astype(jnp.bfloat16),
-        "head",
-        scatter_dimension=0,
-        tiled=True,
-    )
+    dec_part = jnp.dot(dec_attended, out_weight, preferred_element_type=jnp.float32).astype(jnp.bfloat16)
+    heads = lax.axis_size("head")
+    pad_rows = 16
+    dec_part = dec_part.reshape(heads, DEC // heads, D)
+    dec_part = jnp.pad(dec_part, ((0, 0), (0, pad_rows - DEC // heads), (0, 0)))
+    both = jnp.concatenate([stretch_part.reshape(heads, rows_own, D), dec_part], axis=1)
+    summed = lax.psum_scatter(
+        both.reshape(heads * (rows_own + pad_rows), D), "head", scatter_dimension=0, tiled=True
+    )
+    stretch_out = summed[:rows_own]
+    decode_out = summed[rows_own : rows_own + DEC // heads]
     return (stretch_out[None], decode_out[None], state_next[None])
 
 

time: 306 us -> 200 us (0.65)
  waiting for transfers between devices: 227 us -> 130 us
  starting transfers between devices: 30.4 us -> 25.2 us
  matrix products: 15.7 us -> 12.1 us
    unnamed x4 -> x2, waiting for transfers between devices: 104 us -> 0.03 us
    all_gather x1, waiting for transfers between devices: 0.02 us -> 16.7 us  [local(): lax.all_gather(conved, 'head', axis=0, tiled=True)]
    all_to_all x1 -> x0, starting transfers between devices: 16.6 us -> none  [local(): lax.all_to_all(sent_slots, 'tok', split_axis=0, concat_axis=0, tiled=True)]
    all_to_all x1, starting transfers between devices: 5.13 us -> 16.6 us  [local(): lax.all_to_all(sent_rows, 'tok', split_axis=0, concat_axis=0, tiled=True)]
    all_to_all x1 -> x0, waiting for transfers between devices: 7.05 us -> none  [local(): lax.all_to_all(sent_slots, 'tok', split_axis=0, concat_axis=0, tiled=True)]
    concatenate x0 -> x2, other arithmetic: none -> 3.12 us  [the longest x1 2.41 us: local(): jnp.concatenate([stretch_part.reshape(heads, rows_own, D), dec_part], axi...]
  transfers between devices with their start and end apart: 7 -> 5, of which waited for: 5 -> 4; matrix products, arithmetic and copies ran while one was open for 9% -> 5% of each run, Pallas kernels for 0% -> 0%
where the time goes in v1:
time: 200 us; the launch traced here: 199 us
  waiting for transfers between devices  130 us (65%)
  starting transfers between devices  25.2 us (13%)
  between operations  15.8 us (8%)
  matrix products  12.1 us (6%)
  other arithmetic  9.77 us (5%)
  local copies, waits for them, and re-layouts  6 us (3%)
    reduce_scatter x1, waiting for transfers between devices, local(): lax.psum_scatter(both.reshape(heads * (rows_own + pad_rows), D), 'head',...  91.2 us
    all_gather x1, waiting for transfers between devices, local(): lax.all_gather(conved, 'head', axis=0, tiled=True)  16.7 us
    all_to_all x1, starting transfers between devices, local(): lax.all_to_all(sent_rows, 'tok', split_axis=0, concat_axis=0, tiled=True)  16.6 us
    all_to_all x1, waiting for transfers between devices, local(): lax.all_to_all(served, 'tok', split_axis=0, concat_axis=0, tiled=True)  11.7 us
    all_to_all x1, waiting for transfers between devices, local(): lax.all_to_all(sent_rows, 'tok', split_axis=0, concat_axis=0, tiled=True)  10.7 us
    all_to_all x1, starting transfers between devices, local(): lax.all_to_all(served, 'tok', split_axis=0, concat_axis=0, tiled=True)  4.62 us
  transfers between devices with their start and end apart: 5, of which 4 were waited for; matrix products, arithmetic and copies ran while one was open for 5% of the time, Pallas kernels for 0%

profile of v1, /device:TPU:1, one launch (start us, length us, event | category | flops | bytes accessed | tf_op | source)
XLA Modules:
  0.0 199.2 jit_solution(16442440949846528474)
XLA Ops:
  7.3 1.2 fusion.39
  8.5 1.1 fusion.41
  9.6 3.9 %collective-permute-start = (bf16[2,1792]{1,0:T(2,128)(2,1)S(1)}, bf16[2,1792]{1,0:T(2,128)(2,1)S(1)}, u32[]{:S(2)}, u32[]{:S(2)}) collective-permute-start(bf16[2,1792]{1,0:T(2,128)(2,1)S(1)} %slice.116), channel_id=1, source_target_pairs={{0,32},{32,64},{64,96},{96,128},{128,160},{160,192},{192,224},{224... | collective-permute-start | bytes 21512 | tf_op jit(solution)/shard_map/ppermute | solution.py:18
  13.6 0.9 slice_reduce_fusion.2
  14.5 0.7 broadcast_select_fusion
  15.3 0.8 fusion.43
  16.2 0.2 convert_reduce_fusion.1
  17.0 0.4 convolution_convert_fusion.3
  17.5 0.7 pad_maximum_fusion
  18.2 16.6 %all-to-all-start = ((bf16[32,2,145]{2,1,0:T(2,128)(2,1)}), bf16[32,2,145]{2,1,0:T(2,128)(2,1)S(1)}, u32[]{:S(2)}, u32[]{:S(2)}) async-start(bf16[32,2,145]{2,1,0:T(2,128)(2,1)} %pad_maximum_fusion), calls=%async_computation | async-start | bytes 65536 | tf_op jit(solution)/shard_map/all_to_all | solution.py:159
  36.1 10.7 %all-to-all-done = bf16[32,2,145]{2,1,0:T(2,128)(2,1)S(1)} async-done(((bf16[32,2,145]{2,1,0:T(2,128)(2,1)}), bf16[32,2,145]{2,1,0:T(2,128)(2,1)S(1)}, u32[]{:S(2)}, u32[]{:S(2)}) %all-to-all-start) | async-done | bytes 18592 | tf_op jit(solution)/shard_map/all_to_all | solution.py:159
  46.8 0.7 convert_reduce_fusion
  48.0 0.7 copy.42
  48.8 2.6 %fusion.2 = f32[64,16,112]{2,0,1:T(8,128)S(1)} fusion(f32[1,16,1,112,273]{3,2,4,1,0:T(1,128)S(1)} %copy-done.1, f32[64,1,256]{2,0,1:T(8,128)} %copy.42, f32[64,1,16]{2,0,1:T(8,128)S(1)} %get-tuple-element.20, f32[273]{0:T(512)S(1)} %pad.10.clone), kind=kOutput, calls=%fused_computation.4 | convolution fusion | flops 375752832 | bytes 2486340 | tf_op jit(solution)/shard_map/nhp,shdp->nshd/dot_general | solution.py:52
  51.5 0.7 fusion.27
  52.2 0.2 multiply_reduce_fusion.1
  52.4 0.7 multiply_convert_fusion
  53.1 4.6 %all-to-all-start.1 = ((bf16[32,2,112]{2,1,0:T(2,128)(2,1)}), bf16[32,2,112]{2,1,0:T(2,128)(2,1)S(1)}, u32[]{:S(2)}, u32[]{:S(2)}) async-start(bf16[32,2,112]{2,1,0:T(2,128)(2,1)} %bitcast.39), calls=%async_computation.1 | async-start | bytes 32768 | tf_op jit(solution)/shard_map/all_to_all | solution.py:171
  57.8 11.7 %all-to-all-done.1 = bf16[32,2,112]{2,1,0:T(2,128)(2,1)S(1)} async-done(((bf16[32,2,112]{2,1,0:T(2,128)(2,1)}), bf16[32,2,112]{2,1,0:T(2,128)(2,1)S(1)}, u32[]{:S(2)}, u32[]{:S(2)}) %all-to-all-start.1) | async-done | bytes 14368 | tf_op jit(solution)/shard_map/all_to_all | solution.py:171
  69.5 0.4 convolution_convert_fusion.1
  70.0 16.7 %all-gather.2.cloned.1.call-done = bf16[1024,1792]{1,0:T(8,128)(2,1)} async-done(((bf16[64,1792]{1,0:T(8,128)(2,1)}), bf16[1024,1792]{1,0:T(8,128)(2,1)}) %all-gather.2.cloned.1.call-update) | async-done | bytes 3670032 | tf_op jit(solution)/shard_map/all_gather | solution.py:90
  86.6 3.4 %fusion.8 = bf16[1024,1,144]{0,2,1:T(8,128)(2,1)S(1)} fusion(bf16[1024,1792]{1,0:T(8,128)(2,1)} %all-gather.2.cloned.1.call-done, bf16[1792,1,144]{0,2,1:T(8,128)(2,1)S(1)} %copy-done), kind=kOutput, calls=%fused_computation.15 | convolution fusion | flops 528629760 | bytes 4481024 | tf_op jit(solution)/shard_map/dot_general | solution.py:89
  90.1 1.1 fusion.9
  91.3 0.7 convolution_bitcast_fusion.1
  92.0 1.2 multiply_reduce_fusion
  93.2 1.2 convolution_convert_fusion
  94.4 2.4 %fusion.1 = bf16[16,80,1792]{2,1,0:T(8,128)(2,1)} fusion(bf16[16,2,1792]{2,1,0:T(2,128)(2,1)S(1)} %reshape.515, bf16[16,64,1792]{2,1,0:T(8,128)(2,1)S(1)} %bitcast.135), kind=kLoop, calls=%fused_computation.2 | loop fusion | flops 13762560 | bytes 8372224 | tf_op jit(solution)/shard_map/concatenate | solution.py:182
  97.0 0.4 fusion.14
  97.4 0.8 copy.45
  98.2 91.2 %reduce-scatter.2.cloned.1.call-done = bf16[80,1792]{1,0:T(8,128)(2,1)} async-done(((bf16[1280,1792]{1,0:T(8,128)(2,1)}), bf16[80,1792]{1,0:T(8,128)(2,1)}) %reduce-scatter.2.cloned.1.call-update) | async-done | bytes 286736 | tf_op jit(solution)/shard_map/reduce_scatter | solution.py:183
  189.4 1.3 slice_bitcast_fusion.16
  190.7 1.6 slice_bitcast_fusion
  (63 shorter events, 1.7 us)
Async XLA Ops:
  7.2 9.8 %copy-start = (bf16[1792,1,144]{0,2,1:T(8,128)(2,1)S(1)}, bf16[1792,1,144]{0,2,1:T(8,128)(2,1)}, u32[]{:S(2)}) copy-start(bf16[1792,1,144]{0,2,1:T(8,128)(2,1)} %param.20) | copy-start | bytes 1548292
  7.2 9.7 %copy-start.5 = (f32[1792]{0:T(1024)S(1)}, f32[1792]{0:T(1024)}, u32[]{:S(2)}) copy-start(f32[1792]{0:T(1024)} %param.18) | copy-start | bytes 21508
  7.2 9.0 %copy-start.9 = (s32[1,32,1]{1,2,0:T(1,128)S(1)}, s32[1,32,1]{1,2,0:T(1,128)}, u32[]{:S(2)}) copy-start(s32[1,32,1]{1,2,0:T(1,128)} %param.27) | copy-start | bytes 388
  7.2 9.1 %copy-start.8 = (s32[1,32]{1,0:T(1,128)S(1)}, s32[1,32]{1,0:T(1,128)}, u32[]{:S(2)}) copy-start(s32[1,32]{1,0:T(1,128)} %param.26) | copy-start | bytes 388
  7.2 9.4 %copy-start.4 = (bf16[1,32,2,1792]{3,2,1,0:T(2,128)(2,1)S(1)}, bf16[1,32,2,1792]{3,2,1,0:T(2,128)(2,1)}, u32[]{:S(2)}) copy-start(bf16[1,32,2,1792]{3,2,1,0:T(2,128)(2,1)} %param.17) | copy-start | bytes 688132
  7.2 9.5 %copy-start.3 = (bf16[1,32,1792]{2,1,0:T(8,128)(2,1)S(1)}, bf16[1,32,1792]{2,1,0:T(8,128)(2,1)}, u32[]{:S(2)}) copy-start(bf16[1,32,1792]{2,1,0:T(8,128)(2,1)} %param.16) | copy-start | bytes 344068
  7.2 79.4 %all-gather.2.cloned.1.call-start = ((), (), s32[]{:S(2)}) async-start(), calls=%async_computation.3 | async-start | bytes 3899392 | tf_op jit(solution)/shard_map/all_gather | solution.py:90
  9.6 4.9 %collective-permute-start = (bf16[2,1792]{1,0:T(2,128)(2,1)S(1)}, bf16[2,1792]{1,0:T(2,128)(2,1)S(1)}, u32[]{:S(2)}, u32[]{:S(2)}) collective-permute-start(bf16[2,1792]{1,0:T(2,128)(2,1)S(1)} %slice.116), channel_id=1, source_target_pairs={{0,32},{32,64},{64,96},{96,128},{128,160},{160,192},{192,224},{224... | collective-permute-start | bytes 21512 | tf_op jit(solution)/shard_map/ppermute | solution.py:18
  15.3 20.8 %copy-start.1 = (f32[1,16,1,112,273]{3,2,4,1,0:T(1,128)S(1)}, f32[1,16,1,112,273]{3,2,4,1,0:T(1,128)}, u32[]{:S(2)}) copy-start(f32[1,16,1,112,273]{3,2,4,1,0:T(1,128)} %param.23) | copy-start | bytes 5870596
  18.2 28.7 %all-to-all-start = ((bf16[32,2,145]{2,1,0:T(2,128)(2,1)}), bf16[32,2,145]{2,1,0:T(2,128)(2,1)S(1)}, u32[]{:S(2)}, u32[]{:S(2)}) async-start(bf16[32,2,145]{2,1,0:T(2,128)(2,1)} %pad_maximum_fusion), calls=%async_computation | async-start | bytes 65536 | tf_op jit(solution)/shard_map/all_to_all | solution.py:159
  36.1 16.2 %copy-start.7 = (f32[112]{0:T(128)S(1)}, f32[112]{0:T(128)}, u32[]{:S(2)}) copy-start(f32[112]{0:T(128)} %param.21) | copy-start | bytes 1348
  47.6 21.9 %copy-start.2 = (bf16[112,1792]{1,0:T(8,128)(2,1)S(1)}, bf16[112,1792]{1,0:T(8,128)(2,1)}, u32[]{:S(2)}) copy-start(bf16[112,1792]{1,0:T(8,128)(2,1)} %param.22) | copy-start | bytes 1204228
  53.1 16.5 %all-to-all-start.1 = ((bf16[32,2,112]{2,1,0:T(2,128)(2,1)}), bf16[32,2,112]{2,1,0:T(2,128)(2,1)S(1)}, u32[]{:S(2)}, u32[]{:S(2)}) async-start(bf16[32,2,112]{2,1,0:T(2,128)(2,1)} %bitcast.39), calls=%async_computation.1 | async-start | bytes 32768 | tf_op jit(solution)/shard_map/all_to_all | solution.py:171
  57.7 131.7 %reduce-scatter.2.cloned.1.call-start = ((), (), s32[]{:S(2)}) async-start(), calls=%async_computation.4 | async-start | bytes 4874240 | tf_op jit(solution)/shard_map/reduce_scatter | solution.py:183
  57.8 32.2 %copy-start.6 = (s32[1024]{0:T(1024)}, s32[1024]{0:T(1024)S(1)}, u32[]{:S(2)}) copy-start(s32[1024]{0:T(1024)S(1)} %iota.31) | copy-start | bytes 12292
  90.0 1.2 slice-start
Sparse Core Ops, SparseCore 0:
  16.3 70.3 all-gather.1
  97.0 92.3 reduce-scatter.1

commit v2 on v1

--- a/solution.py
+++ b/solution.py
@@ -1,8 +1,11 @@
+import functools
 import math
 
 import jax
 import jax.numpy as jnp
 from jax import lax
+from jax.experimental import pallas as pl
+from jax.experimental.pallas import tpu as pltpu
 from jax.sharding import PartitionSpec as P
 
 D = 1792
@@ -10,6 +13,293 @@
 F = 16
 STRETCH = 1024
 DEC = 32
+
+
+SIDE = 4
+MESH = pl.DeviceIdType.MESH
+
+
+def plane_position():
+    me = lax.axis_index("head")
+    return me, lax.rem(me, SIDE), lax.div(me, SIDE)
+
+
+def block_at(half, first, second, mx, my):
+    dx, dy = (first, second) if half == 0 else (second, first)
+    return lax.rem(my + dy % SIDE, SIDE) * SIDE + lax.rem(mx + dx % SIDE, SIDE)
+
+
+def half_rows(half, quarter, rows):
+    start = half * (rows // 2)
+    if quarter is None:
+        return pl.ds(start, rows // 2)
+    return pl.ds(start + quarter * (rows // 4), rows // 4)
+
+
+def greet(peers):
+    barrier = pltpu.get_barrier_semaphore()
+    for peer in peers:
+        pl.semaphore_signal(barrier, inc=1, device_id={"head": peer}, device_id_type=MESH)
+    pl.semaphore_wait(barrier, len(peers))
+
+
+def gather_kernel(own_ref, w_ref, qkv_ref, buf, send_sem, recv_sem):
+    me, mx, my = plane_position()
+    rows = own_ref.shape[0]
+    greet([block_at(0, d, 0, mx, my) for d in (1, -1)] + [block_at(0, 0, d, mx, my) for d in (1, -1)])
+    sent = []
+
+    def send(half, first, second, along_first, step, quarter=None):
+        target = block_at(half, step if along_first else 0, 0 if along_first else step, mx, my)
+        there = ((first - step) % SIDE, second) if along_first else (first, (second - step) % SIDE)
+        block = block_at(half, first, second, mx, my)
+        span = half_rows(half, quarter, rows)
+        own = first == 0 and second == 0
+        slot = half * 16 + there[0] * SIDE + there[1]
+        copy = pltpu.make_async_remote_copy(
+            src_ref=own_ref.at[span] if own else buf.at[block, span],
+            dst_ref=buf.at[block, span],
+            send_sem=send_sem.at[len(sent)],
+            recv_sem=recv_sem.at[slot, quarter or 0],
+            device_id={"head": target},
+            device_id_type=MESH,
+        )
+        copy.start()
+        sent.append(copy)
+
+    def arrived(half, first, second, quarter=None):
+        first, second = first % SIDE, second % SIDE
+        place = buf.at[block_at(half, first, second, mx, my), half_rows(half, quarter, rows)]
+        pltpu.make_async_remote_copy(
+            src_ref=place,
+            dst_ref=place,
+            send_sem=send_sem.at[0],
+            recv_sem=recv_sem.at[half * 16 + first * SIDE + second, quarter or 0],
+            device_id={"head": block_at(0, 1, 0, mx, my)},
+            device_id_type=MESH,
+        ).wait_recv()
+
+    def project(block, value):
+        product = jnp.dot(value, w_ref[...], preferred_element_type=jnp.float32)
+        qkv_ref[pl.ds(pl.multiple_of(block * rows, rows), rows), :] = product.astype(jnp.bfloat16)
+
+    for along_first in (False, True):
+        for half in (0, 1):
+            for step in (1, -1):
+                send(half, 0, 0, along_first, step)
+    project(me, own_ref[...])
+    for step in (1, -1):
+        for half in (0, 1):
+            origin = -step % SIDE
+            arrived(half, origin, 0)
+            send(half, origin, 0, True, step, 0 if step == 1 else 1)
+            for out in (1, -1):
+                send(half, origin, 0, False, out)
+
+    def pass_on(half, first):
+        for step in (1, -1):
+            origin = -step % SIDE
+            arrived(half, first, origin)
+            send(half, first, origin, False, step, 0 if step == 1 else 1)
+
+    for half in (0, 1):
+        pass_on(half, 0)
+    for half in (0, 1):
+        for quarter in (0, 1):
+            arrived(half, 2, 0, quarter)
+        for out in (1, -1):
+            send(half, 2, 0, False, out)
+    for first in (3, 1, 2):
+        for half in (0, 1):
+            pass_on(half, first)
+    for dx in (1, 3, 0):
+        for dy in (1, 3, 0):
+            if dx or dy:
+                block = block_at(0, dx, dy, mx, my)
+                project(block, buf[block])
+    for first in (0, 3, 1, 2):
+        for half in (0, 1):
+            for quarter in (0, 1):
+                arrived(half, first, 2, quarter)
+        for dx, dy in {(first, 2), (2, first)}:
+            block = block_at(0, dx, dy, mx, my)
+            project(block, buf[block])
+    for copy in sent:
+        copy.wait_send()
+
+
+def gather_project(conved, weight):
+    rows, width = conved.shape
+    columns = weight.shape[1]
+    whole = pl.BlockSpec(memory_space=pltpu.VMEM)
+    return pl.pallas_call(
+        gather_kernel,
+        out_shape=jax.ShapeDtypeStruct((16 * rows, columns), jnp.bfloat16),
+        in_specs=[whole, whole],
+        out_specs=whole,
+        scratch_shapes=[
+            pltpu.VMEM((16, rows, width), jnp.bfloat16),
+            pltpu.SemaphoreType.DMA((40,)),
+            pltpu.SemaphoreType.DMA((32, 2)),
+        ],
+        compiler_params=pltpu.CompilerParams(
+            collective_id=0, has_side_effects=True, vmem_limit_bytes=40 * 2**20
+        ),
+        name="gather_project",
+    )(conved, weight)
+
+
+def scatter_kernel(
+    rows, att_ref, w_ref, dec_ref, out_ref, dec_out_ref,
+    part, far, near, far_last, near_last, dec_in, send_sem, far_sem, near_sem, dec_send, dec_recv,
+):
+    me, mx, my = plane_position()
+    peers = [lax.rem(me + k, 16) for k in range(1, 16)]
+    greet(peers)
+    dec_copies = []
+    for k, peer in enumerate(peers):
+        copy = pltpu.make_async_remote_copy(
+            src_ref=dec_ref.at[peer],
+            dst_ref=dec_in.at[k],
+            send_sem=dec_send.at[k],
+            recv_sem=dec_recv.at[k],
+            device_id={"head": peer},
+            device_id_type=MESH,
+        )
+        copy.start()
+        dec_copies.append(copy)
+    sent = []
+
+    def send(half, along_first, step, source, target_ref, sem):
+        copy = pltpu.make_async_remote_copy(
+            src_ref=source,
+            dst_ref=target_ref,
+            send_sem=send_sem.at[len(sent)],
+            recv_sem=sem,
+            device_id={
+                "head": block_at(half, step if along_first else 0, 0 if along_first else step, mx, my)
+            },
+            device_id_type=MESH,
+        )
+        copy.start()
+        sent.append(copy)
+
+    def arrived(place, sem):
+        pltpu.make_async_remote_copy(
+            src_ref=place,
+            dst_ref=place,
+            send_sem=send_sem.at[0],
+            recv_sem=sem,
+            device_id={"head": block_at(0, 1, 0, mx, my)},
+            device_id_type=MESH,
+        ).wait_recv()
+
+    def project(dx, dy):
+        block = block_at(0, dx, dy, mx, my)
+        value = att_ref[pl.ds(pl.multiple_of(block * rows, rows), rows), :]
+        product = jnp.dot(value, w_ref[...], preferred_element_type=jnp.float32)
+        part[block] = product.astype(jnp.bfloat16)
+
+    def piece(half, first, second, quarter=None):
+        return block_at(half, first, second, mx, my), half_rows(half, quarter, rows)
+
+    def wide(value):
+        return value.astype(jnp.float32)
+
+    def send_far(half, first):
+        for quarter, step in ((0, -1), (1, 1)):
+            block, span = piece(half, first, 2, quarter)
+            slot = half * SIDE + first
+            send(half, False, step, part.at[block, span], far.at[slot, quarter], far_sem.at[slot, quarter])
+
+    order = (2, 1, 3, 0)
+    for first in order:
+        for dx, dy in sorted({(first, 2), (2, first)}):
+            project(dx, dy)
+        for half in (0, 1):
+            send_far(half, first)
+    for dx in (1, 3, 0):
+        for dy in (1, 3, 0):
+            project(dx, dy)
+    for first in order:
+        for half in (0, 1):
+            slot = half * SIDE + first
+            for quarter, step in ((0, -1), (1, 1)):
+                arrived(far.at[slot, quarter], far_sem.at[slot, quarter])
+                block, span = piece(half, first, step, quarter)
+                part[block, span, :] = (wide(part[block, span, :]) + wide(far[slot, quarter])).astype(jnp.bfloat16)
+                block, span = piece(half, first, step)
+                send(half, False, step, part.at[block, span], near.at[slot, quarter], near_sem.at[slot, quarter])
+    for first in order:
+        for half in (0, 1):
+            slot = half * SIDE + first
+            for quarter in (0, 1):
+                arrived(near.at[slot, quarter], near_sem.at[slot, quarter])
+            block, span = piece(half, first, 0)
+            if first == 0:
+                continue
+            total = wide(part[block, span, :]) + wide(near[slot, 0]) + wide(near[slot, 1])
+            part[block, span, :] = total.astype(jnp.bfloat16)
+            if first == 2:
+                for quarter, step in ((0, -1), (1, 1)):
+                    block, span = piece(half, 2, 0, quarter)
+                    send(half, True, step, part.at[block, span], far_last.at[half, quarter], far_sem.at[8 + half, quarter])
+            else:
+                quarter, step = (1, 1) if first == 1 else (0, -1)
+                arrived(far_last.at[half, quarter], far_sem.at[8 + half, quarter])
+                inner, inner_span = piece(half, step, 0, quarter)
+                part[inner, inner_span, :] = (
+                    wide(part[inner, inner_span, :]) + wide(far_last[half, quarter])
+                ).astype(jnp.bfloat16)
+                send(half, True, step, part.at[block, span], near_last.at[half, quarter], near_sem.at[8 + half, quarter])
+    dec_total = wide(dec_ref[me])
+    for k, copy in enumerate(dec_copies):
+        copy.wait_recv()
+        dec_total = dec_total + wide(dec_in[k])
+    dec_out_ref[...] = dec_total.astype(jnp.bfloat16)
+    for half in (0, 1):
+        block, span = piece(half, 0, 0)
+        total = wide(part[block, span, :]) + wide(near[half * SIDE, 0]) + wide(near[half * SIDE, 1])
+        for quarter in (0, 1):
+            arrived(near_last.at[half, quarter], near_sem.at[8 + half, quarter])
+            total = total + wide(near_last[half, quarter])
+        out_ref[span, :] = total.astype(jnp.bfloat16)
+    for copy in sent:
+        copy.wait_send()
+    for copy in dec_copies:
+        copy.wait_send()
+
+
+def project_scatter(attended, weight, dec_parts):
+    rows = attended.shape[0] // 16
+    width = weight.shape[1]
+    whole = pl.BlockSpec(memory_space=pltpu.VMEM)
+    return pl.pallas_call(
+        functools.partial(scatter_kernel, rows),
+        out_shape=(
+            jax.ShapeDtypeStruct((rows, width), jnp.bfloat16),
+            jax.ShapeDtypeStruct(dec_parts.shape[1:], jnp.bfloat16),
+        ),
+        in_specs=[whole, whole, whole],
+        out_specs=(whole, whole),
+        scratch_shapes=[
+            pltpu.VMEM((16, rows, width), jnp.bfloat16),
+            pltpu.VMEM((8, 2, rows // 4, width), jnp.bfloat16),
+            pltpu.VMEM((8, 2, rows // 2, width), jnp.bfloat16),
+            pltpu.VMEM((2, 2, rows // 4, width), jnp.bfloat16),
+            pltpu.VMEM((2, 2, rows // 2, width), jnp.bfloat16),
+            pltpu.VMEM((15,) + dec_parts.shape[1:], jnp.bfloat16),
+            pltpu.SemaphoreType.DMA((40,)),
+            pltpu.SemaphoreType.DMA((10, 2)),
+            pltpu.SemaphoreType.DMA((10, 2)),
+            pltpu.SemaphoreType.DMA((15,)),
+            pltpu.SemaphoreType.DMA((15,)),
+        ],
+        compiler_params=pltpu.CompilerParams(
+            collective_id=1, has_side_effects=True, vmem_limit_bytes=40 * 2**20
+        ),
+        name="project_scatter",
+    )(attended, weight, dec_parts)
 
 
 def from_behind(array, axis, by):
@@ -86,11 +376,7 @@
     first_dev = lax.axis_index("head") == 0
     rim_rows = jnp.where(first_dev, stretch_tail[0], rim_rows)
     conved = convolve(rim_rows, normed, conv_taps)
-    grouped = jnp.dot(
-        lax.all_gather(conved, "head", axis=0, tiled=True),
-        w_flat,
-        preferred_element_type=jnp.float32,
-    ).astype(jnp.bfloat16)
+    grouped = gather_project(conved, w_flat)
     grouped = grouped.reshape(STRETCH, head_count, block_width)
     queries = grouped[:, :, :F]
     key_feats = grouped[:, :, F : 2 * F]
@@ -136,7 +422,6 @@
     state_next = state_old + jnp.einsum(
         "jhd,jhp->hdp", values, key_phi, preferred_element_type=jnp.float32
     )
-    stretch_part = jnp.dot(attended, out_weight, preferred_element_type=jnp.float32).astype(jnp.bfloat16)
     dec_normed = rms_rows(decode_tokens[0], norm_gain).astype(jnp.bfloat16)
     dec_conved = convolve(decode_tail[0], dec_normed[:, None, :], conv_taps)[:, 0, :]
     dec_qkv = jnp.dot(dec_conved, w_flat, preferred_element_type=jnp.float32).astype(jnp.bfloat16)
@@ -176,15 +461,12 @@
     ).astype(jnp.bfloat16)
     dec_part = jnp.dot(dec_attended, out_weight, preferred_element_type=jnp.float32).astype(jnp.bfloat16)
     heads = lax.axis_size("head")
-    pad_rows = 16
-    dec_part = dec_part.reshape(heads, DEC // heads, D)
-    dec_part = jnp.pad(dec_part, ((0, 0), (0, pad_rows - DEC // heads), (0, 0)))
-    both = jnp.concatenate([stretch_part.reshape(heads, rows_own, D), dec_part], axis=1)
-    summed = lax.psum_scatter(
-        both.reshape(heads * (rows_own + pad_rows), D), "head", scatter_dimension=0, tiled=True
-    )
-    stretch_out = summed[:rows_own]
-    decode_out = summed[rows_own : rows_own + DEC // heads]
+    lanes = 128
+    dec_part = dec_part.reshape(heads, DEC // heads * D // lanes, lanes)
+    used = dec_part.shape[1]
+    dec_part = jnp.pad(dec_part, ((0, 0), (0, -used % 16), (0, 0)))
+    stretch_out, dec_sum = project_scatter(attended, out_weight, dec_part)
+    decode_out = dec_sum[:used].reshape(DEC // heads, D)
     return (stretch_out[None], decode_out[None], state_next[None])
 
 

time: 200 us -> 129 us (0.65)
  waiting for transfers between devices: 130 us -> 9.5 us
  Pallas kernels: 0 us -> 54.7 us
  between operations: 15.8 us -> 2.43 us
  starting transfers between devices: 25.2 us -> 34.5 us
  matrix products: 12.1 us -> 9.32 us
    reduce_scatter x1 -> x0, waiting for transfers between devices: 91.2 us -> none  [local(): lax.psum_scatter(both.reshape(heads * (rows_own + pad_rows), D), 'head',...]
    pallas_call x0 -> x2, Pallas kernels: none -> 54.7 us  [the longest x1 28.1 us: project_scatter(): pl.pallas_call(functools.partial(scatter_kernel, rows), out_shape=(jax.Sh...]
    all_gather x1 -> x0, waiting for transfers between devices: 16.7 us -> none  [local(): lax.all_gather(conved, 'head', axis=0, tiled=True)]
    all_to_all x1, waiting for transfers between devices: 10.7 us -> 0.01 us  [local(): lax.all_to_all(sent_rows, 'tok', split_axis=0, concat_axis=0, tiled=True)]
    all_to_all x1, starting transfers between devices: 4.62 us -> 14.3 us  [local(): lax.all_to_all(served, 'tok', split_axis=0, concat_axis=0, tiled=True)]
    dot_general x2 -> x0, matrix products: 4.58 us -> none  [the longest x1 3.36 us: local(): jnp.dot(lax.all_gather(conved, 'head', axis=0, tiled=True), w_flat, prefe...]
    broadcast_in_dim x2 -> x0, local copies, waits for them, and re-layouts: 2.99 us -> none  [local(): return (stretch_out[None], decode_out[None], state_next[None])]
    concatenate x1 -> x0, other arithmetic: 2.41 us -> none  [local(): jnp.concatenate([stretch_part.reshape(heads, rows_own, D), dec_part], axi...]
  transfers between devices with their start and end apart: 5 -> 3, of which waited for: 4 -> 1; matrix products, arithmetic and copies ran while one was open for 5% -> 15% of each run, Pallas kernels for 0% -> 21%
where the time goes in v2:
time: 129 us
  Pallas kernels  54.7 us (42%)
  starting transfers between devices  34.5 us (27%)
  other arithmetic  11 us (9%)
  waiting for transfers between devices  9.5 us (7%)
  matrix products  9.32 us (7%)
  local copies, waits for them, and re-layouts  7.23 us (6%)
  between operations  2.43 us (2%)
    pallas_call x1, Pallas kernels, project_scatter(): pl.pallas_call(functools.partial(scatter_kernel, rows), out_shape=(jax.Sh...  28.1 us
    pallas_call x1, Pallas kernels, gather_project(): pl.pallas_call(gather_kernel, out_shape=jax.ShapeDtypeStruct((16 * rows,...  26.5 us
    all_to_all x1, starting transfers between devices, local(): lax.all_to_all(sent_rows, 'tok', split_axis=0, concat_axis=0, tiled=True)  16.2 us
    all_to_all x1, starting transfers between devices, local(): lax.all_to_all(served, 'tok', split_axis=0, concat_axis=0, tiled=True)  14.3 us
    all_to_all x1, waiting for transfers between devices, local(): lax.all_to_all(served, 'tok', split_axis=0, concat_axis=0, tiled=True)  9.49 us
    ppermute x1, starting transfers between devices, from_behind(): return lax.ppermute(array, axis, pairs)  3.93 us
    dot_general x1, matrix products, local(): jnp.einsum('ihp,hdp->ihd', features(queries.astype(jnp.float32)), state_o...  2.83 us
    unnamed x22, local copies, waits for them, and re-layouts  2.82 us
  transfers between devices with their start and end apart: 3, of which 1 were waited for; matrix products, arithmetic and copies ran while one was open for 15% of the time, Pallas kernels for 21%

profile of v2, /device:TPU:1, one launch (start us, length us, event | category | flops | bytes accessed | tf_op | source)
XLA Modules:
  0.0 128.6 jit_solution(2571075094595434379)
XLA Ops:
  0.6 1.1 fusion.36
  1.8 1.1 fusion.38
  2.9 3.9 %collective-permute-start = (bf16[2,1792]{1,0:T(2,128)(2,1)S(1)}, bf16[2,1792]{1,0:T(2,128)(2,1)S(1)}, u32[]{:S(2)}, u32[]{:S(2)}) collective-permute-start(bf16[2,1792]{1,0:T(2,128)(2,1)S(1)} %slice.112), channel_id=1, source_target_pairs={{0,32},{32,64},{64,96},{96,128},{128,160},{160,192},{192,224},{224... | collective-permute-start | bytes 21512 | tf_op jit(solution)/shard_map/ppermute | solution.py:308
  6.8 0.7 add_bitcast_fusion
  7.5 0.9 convert_reduce_fusion.1
  8.4 0.7 multiply_add_fusion.1
  9.2 1.0 fusion.48
  10.4 0.9 slice_reduce_fusion.2
  11.3 1.0 fusion.47
  12.3 1.0 copy.88
  13.4 0.4 convolution_convert_fusion.1
  13.8 0.7 pad_maximum_fusion
  14.5 16.2 %all-to-all-start = ((bf16[32,2,145]{2,1,0:T(2,128)(2,1)}), bf16[32,2,145]{2,1,0:T(2,128)(2,1)S(1)}, u32[]{:S(2)}, u32[]{:S(2)}) async-start(bf16[32,2,145]{2,1,0:T(2,128)(2,1)} %pad_maximum_fusion), calls=%async_computation | async-start | bytes 65536 | tf_op jit(solution)/shard_map/all_to_all | solution.py:444
  32.0 0.9 constant_dynamic-slice_fusion
  33.6 26.5 %gather_project.1 = bf16[1024,144]{1,0:T(8,128)(2,1)S(1)} custom-call(bf16[64,1792]{1,0:T(8,128)(2,1)S(1)} %fusion.40.own_ref, bf16[1792,144]{1,0:T(8,128)(2,1)S(1)} %bitcast.125), custom_call_target="tpu_custom_call" | custom-call | tf_op jit(solution)/shard_map/gather_project/pallas_call | solution.py:135
  60.4 1.1 fusion.6
  62.2 0.7 convolution_bitcast_fusion.1
  62.9 2.8 %multiply_reduce_fusion = (f32[1024]{0:T(1024)S(1)}, f32[1024,1,112]{2,0,1:T(8,128)S(1)}) fusion(f32[512,1,112]{2,0,1:T(8,128)S(1)} %fusion.6, f32[512,1,112]{2,0,1:T(8,128)S(1)} %convolution_bitcast_fusion.1, f32[1024,1,256]{0,2,1:T(8,128)S(1)} %bitcast.133, f32[1024,1,16]{0,2,1:T(8,128)S(1)} %copy.49, f32[273]{0:T(512)S(1)} %pad.17.clone, ...), kind=kOutput, calls=%fused_computation.47 | convolution fusion | flops 376734720 | bytes 2159108 | tf_op jit(solution)/shard_map/ihp,hdp->ihd/dot_general | solution.py:388
  66.1 0.9 multiply_multiply_fusion
  67.0 0.7 copy.62
  67.8 0.7 convert_reduce_fusion
  69.1 1.8 %fusion = f32[64,16,112]{2,0,1:T(8,128)S(1)} fusion(f32[1,16,1,112,273]{3,2,4,1,0:T(1,128)S(1)} %copy-done.1, f32[64,1,256]{2,0,1:T(8,128)S(1)} %copy.57, f32[64,1,16]{2,0,1:T(8,128)S(1)} %get-tuple-element.24, f32[273]{0:T(512)S(1)} %pad.17.clone), kind=kOutput, calls=%fused_computation | convolution fusion | flops 375752832 | bytes 2486340 | tf_op jit(solution)/shard_map/nhp,shdp->nshd/dot_general | solution.py:342
  71.0 0.7 fusion.25
  71.8 0.7 multiply_convert_fusion
  72.5 14.3 %all-to-all-start.1 = ((bf16[32,2,112]{2,1,0:T(2,128)(2,1)}), bf16[32,2,112]{2,1,0:T(2,128)(2,1)S(1)}, u32[]{:S(2)}, u32[]{:S(2)}) async-start(bf16[32,2,112]{2,1,0:T(2,128)(2,1)} %bitcast.38), calls=%async_computation.1 | async-start | bytes 32768 | tf_op jit(solution)/shard_map/all_to_all | solution.py:456
  86.9 1.4 %fusion.11 = f32[1,1,112,273]{2,3,1,0:T(8,128)S(1)} fusion(bf16[1024,1,1,1,1,1,256]{0,6,5,4,3,2,1:T(8,128)(2,1)} %bitcast.135, bf16[1024,1,1,1,1,1,16]{0,6,5,4,3,2,1:T(8,128)(2,1)S(1)} %copy-done.3, f32[273]{0:T(512)S(1)} %pad.17.clone, pred[1024]{0:T(1024)(128)(4,1)S(1)} %copy-done.8, bf16[1024,1,144]{2,0,1:T(8,128)(2,1)S(1)} %bitcast.130, ...), kind=kOutput, calls=%fused_computation.19 | convolution fusion | flops 64607088 | bytes 1084352 | tf_op jit(solution)/shard_map/jhd,jhp->hdp/dot_general | solution.py:422
  88.3 0.8 copy.63
  89.1 9.5 %all-to-all-done.1 = bf16[32,2,112]{2,1,0:T(2,128)(2,1)S(1)} async-done(((bf16[32,2,112]{2,1,0:T(2,128)(2,1)}), bf16[32,2,112]{2,1,0:T(2,128)(2,1)S(1)}, u32[]{:S(2)}, u32[]{:S(2)}) %all-to-all-start.1) | async-done | bytes 14368 | tf_op jit(solution)/shard_map/all_to_all | solution.py:456
  98.6 0.4 convolution_convert_fusion
  99.2 28.1 %project_scatter.1 = (bf16[64,1792]{1,0:T(8,128)(2,1)S(1)}, bf16[32,128]{1,0:T(8,128)(2,1)S(1)}) custom-call(bf16[1024,112]{1,0:T(8,128)(2,1)S(1)} %fusion.42.att_ref, bf16[112,1792]{1,0:T(8,128)(2,1)S(1)} %copy-done, bf16[16,32,128]{2,1,0:T(8,128)(2,1)S(1)} %pad.4.dec_ref), custom_call_target="tpu_custom_call" | custom-call | tf_op jit(solution)/shard_map/project_scatter/pallas_call | solution.py:277
  127.3 0.6 broadcast_in_dim_reshape.2
  127.9 0.7 copy.93
  (62 shorter events, 3.2 us)
Async XLA Ops:
  0.6 12.7 %copy-start.2 = (bf16[1792,1,144]{0,2,1:T(8,128)(2,1)S(1)}, bf16[1792,1,144]{0,2,1:T(8,128)(2,1)}, u32[]{:S(2)}) copy-start(bf16[1792,1,144]{0,2,1:T(8,128)(2,1)} %param.20) | copy-start | bytes 1548292
  2.9 30.5 %collective-permute-start = (bf16[2,1792]{1,0:T(2,128)(2,1)S(1)}, bf16[2,1792]{1,0:T(2,128)(2,1)S(1)}, u32[]{:S(2)}, u32[]{:S(2)}) collective-permute-start(bf16[2,1792]{1,0:T(2,128)(2,1)S(1)} %slice.112), channel_id=1, source_target_pairs={{0,32},{32,64},{64,96},{96,128},{128,160},{160,192},{192,224},{224... | collective-permute-start | bytes 21512 | tf_op jit(solution)/shard_map/ppermute | solution.py:308
  12.3 21.1 %copy-start.5 = (bf16[1,2,1792]{2,1,0:T(2,128)(2,1)S(1)}, bf16[1,2,1792]{2,1,0:T(2,128)(2,1)}, u32[]{:S(2)}) copy-start(bf16[1,2,1792]{2,1,0:T(2,128)(2,1)} %param.15) | copy-start | bytes 21508
  14.5 53.2 %all-to-all-start = ((bf16[32,2,145]{2,1,0:T(2,128)(2,1)}), bf16[32,2,145]{2,1,0:T(2,128)(2,1)S(1)}, u32[]{:S(2)}, u32[]{:S(2)}) async-start(bf16[32,2,145]{2,1,0:T(2,128)(2,1)} %pad_maximum_fusion), calls=%async_computation | async-start | bytes 65536 | tf_op jit(solution)/shard_map/all_to_all | solution.py:444
  33.0 27.4 %copy-start.7 = (pred[1024]{0:T(1024)(128)(4,1)}, pred[1024]{0:T(1024)(128)(4,1)S(1)}, u32[]{:S(2)}) copy-start(pred[1024]{0:T(1024)(128)(4,1)S(1)} %iota_compare_fusion.7) | copy-start | bytes 3076
  33.3 26.9 %copy-start.4 = (s32[1024]{0:T(1024)}, s32[1024]{0:T(1024)S(1)}, u32[]{:S(2)}) copy-start(s32[1024]{0:T(1024)S(1)} %iota.31) | copy-start | bytes 12292
  61.5 0.7 slice-start
  61.5 0.7 slice-start.1
  62.2 3.6 %copy-start.6 = (f32[112]{0:T(128)S(1)}, f32[112]{0:T(128)}, u32[]{:S(2)}) copy-start(f32[112]{0:T(128)} %param.21) | copy-start | bytes 1348
  62.2 3.6 %copy-start.8 = (pred[1024]{0:T(1024)(128)(4,1)S(1)}, pred[1024]{0:T(1024)(128)(4,1)}, u32[]{:S(2)}) copy-start(pred[1024]{0:T(1024)(128)(4,1)} %copy-done.7) | copy-start | bytes 3076
  65.8 3.4 %copy-start.1 = (f32[1,16,1,112,273]{3,2,4,1,0:T(1,128)S(1)}, f32[1,16,1,112,273]{3,2,4,1,0:T(1,128)}, u32[]{:S(2)}) copy-start(f32[1,16,1,112,273]{3,2,4,1,0:T(1,128)} %param.23) | copy-start | bytes 5870596
  68.7 18.1 %copy-start.3 = (bf16[1024,1,1,1,1,1,16]{0,6,5,4,3,2,1:T(8,128)(2,1)S(1)}, bf16[1024,1,1,1,1,1,16]{0,6,5,4,3,2,1:T(8,128)(2,1)}, u32[]{:S(2)}) copy-start(bf16[1024,1,1,1,1,1,16]{0,6,5,4,3,2,1:T(8,128)(2,1)} %copy.62) | copy-start | bytes 98308
  70.9 27.7 %copy-start = (bf16[112,1792]{1,0:T(8,128)(2,1)S(1)}, bf16[112,1792]{1,0:T(8,128)(2,1)}, u32[]{:S(2)}) copy-start(bf16[112,1792]{1,0:T(8,128)(2,1)} %w_ref.1) | copy-start | bytes 1204228
  72.5 26.1 %all-to-all-start.1 = ((bf16[32,2,112]{2,1,0:T(2,128)(2,1)}), bf16[32,2,112]{2,1,0:T(2,128)(2,1)S(1)}, u32[]{:S(2)}, u32[]{:S(2)}) async-start(bf16[32,2,112]{2,1,0:T(2,128)(2,1)} %bitcast.38), calls=%async_computation.1 | async-start | bytes 32768 | tf_op jit(solution)/shard_map/all_to_all | solution.py:456

commit v3 on v2

--- a/solution.py
+++ b/solution.py
@@ -40,13 +40,67 @@
     barrier = pltpu.get_barrier_semaphore()
     for peer in peers:
         pl.semaphore_signal(barrier, inc=1, device_id={"head": peer}, device_id_type=MESH)
-    pl.semaphore_wait(barrier, len(peers))
-
-
-def gather_kernel(own_ref, w_ref, qkv_ref, buf, send_sem, recv_sem):
+    groups, mine = lax.axis_size("tok"), lax.axis_index("tok")
+
+    def hail(k, carry):
+        pl.semaphore_signal(
+            barrier, inc=1, device_id={"tok": lax.rem(mine + k, groups)}, device_id_type=MESH
+        )
+        return carry
+
+    lax.fori_loop(1, groups, hail, 0)
+    return barrier, len(peers) + groups - 1
+
+
+def swap_copy(k, source, landing, send_sem, recv_sem):
+    groups, mine = lax.axis_size("tok"), lax.axis_index("tok")
+    peer = lax.rem(mine + k, groups)
+    return pltpu.make_async_remote_copy(
+        src_ref=source.at[peer],
+        dst_ref=landing.at[mine],
+        send_sem=send_sem.at[k],
+        recv_sem=recv_sem.at[k],
+        device_id={"tok": peer},
+        device_id_type=MESH,
+    )
+
+
+def swap_start(source, landing, send_sem, recv_sem):
+    def body(k, carry):
+        swap_copy(k, source, landing, send_sem, recv_sem).start()
+        return carry
+
+    lax.fori_loop(1, lax.axis_size("tok"), body, 0)
+
+
+def swap_finish(source, landing, send_sem, recv_sem):
+    groups, mine = lax.axis_size("tok"), lax.axis_index("tok")
+
+    def body(k, carry):
+        origin = lax.rem(mine + groups - k, groups)
+        pltpu.make_async_remote_copy(
+            src_ref=landing.at[origin],
+            dst_ref=landing.at[origin],
+            send_sem=send_sem.at[k],
+            recv_sem=recv_sem.at[k],
+            device_id={"tok": lax.rem(mine + k, groups)},
+            device_id_type=MESH,
+        ).wait_recv()
+        swap_copy(k, source, landing, send_sem, recv_sem).wait_send()
+        return carry
+
+    lax.fori_loop(1, groups, body, 0)
+    landing[mine] = source[mine]
+
+
+def gather_kernel(
+    own_ref, w_ref, items_ref, qkv_ref, got_ref, buf, landing, send_sem, recv_sem, swap_send, swap_recv
+):
     me, mx, my = plane_position()
     rows = own_ref.shape[0]
-    greet([block_at(0, d, 0, mx, my) for d in (1, -1)] + [block_at(0, 0, d, mx, my) for d in (1, -1)])
+    barrier, callers = greet(
+        [block_at(0, d, 0, mx, my) for d in (1, -1)] + [block_at(0, 0, d, mx, my) for d in (1, -1)]
+    )
     sent = []
 
     def send(half, first, second, along_first, step, quarter=None):
@@ -83,11 +137,13 @@
         product = jnp.dot(value, w_ref[...], preferred_element_type=jnp.float32)
         qkv_ref[pl.ds(pl.multiple_of(block * rows, rows), rows), :] = product.astype(jnp.bfloat16)
 
+    project(me, own_ref[...])
+    pl.semaphore_wait(barrier, callers)
     for along_first in (False, True):
         for half in (0, 1):
             for step in (1, -1):
                 send(half, 0, 0, along_first, step)
-    project(me, own_ref[...])
+    swap_start(items_ref, landing, swap_send, swap_recv)
     for step in (1, -1):
         for half in (0, 1):
             origin = -step % SIDE
@@ -112,6 +168,8 @@
     for first in (3, 1, 2):
         for half in (0, 1):
             pass_on(half, first)
+    swap_finish(items_ref, landing, swap_send, swap_recv)
+    got_ref[...] = landing[...]
     for dx in (1, 3, 0):
         for dy in (1, 3, 0):
             if dx or dy:
@@ -128,46 +186,41 @@
         copy.wait_send()
 
 
-def gather_project(conved, weight):
+def gather_project(conved, weight, items):
     rows, width = conved.shape
     columns = weight.shape[1]
     whole = pl.BlockSpec(memory_space=pltpu.VMEM)
     return pl.pallas_call(
         gather_kernel,
-        out_shape=jax.ShapeDtypeStruct((16 * rows, columns), jnp.bfloat16),
-        in_specs=[whole, whole],
-        out_specs=whole,
+        out_shape=(
+            jax.ShapeDtypeStruct((16 * rows, columns), jnp.bfloat16),
+            jax.ShapeDtypeStruct(items.shape, items.dtype),
+        ),
+        in_specs=[whole, whole, whole],
+        out_specs=(whole, whole),
         scratch_shapes=[
             pltpu.VMEM((16, rows, width), jnp.bfloat16),
+            pltpu.VMEM(items.shape, items.dtype),
             pltpu.SemaphoreType.DMA((40,)),
             pltpu.SemaphoreType.DMA((32, 2)),
+            pltpu.SemaphoreType.DMA((items.shape[0],)),
+            pltpu.SemaphoreType.DMA((items.shape[0],)),
         ],
         compiler_params=pltpu.CompilerParams(
             collective_id=0, has_side_effects=True, vmem_limit_bytes=40 * 2**20
         ),
         name="gather_project",
-    )(conved, weight)
+    )(conved, weight, items)
 
 
 def scatter_kernel(
-    rows, att_ref, w_ref, dec_ref, out_ref, dec_out_ref,
-    part, far, near, far_last, near_last, dec_in, send_sem, far_sem, near_sem, dec_send, dec_recv,
+    rows, att_ref, w_ref, served_ref, place_ref, out_ref, dec_out_ref,
+    part, far, near, far_last, near_last, landing, dec_wide, dec_ref, dec_in,
+    send_sem, far_sem, near_sem, dec_send, dec_recv, swap_send, swap_recv,
 ):
     me, mx, my = plane_position()
     peers = [lax.rem(me + k, 16) for k in range(1, 16)]
-    greet(peers)
-    dec_copies = []
-    for k, peer in enumerate(peers):
-        copy = pltpu.make_async_remote_copy(
-            src_ref=dec_ref.at[peer],
-            dst_ref=dec_in.at[k],
-            send_sem=dec_send.at[k],
-            recv_sem=dec_recv.at[k],
-            device_id={"head": peer},
-            device_id_type=MESH,
-        )
-        copy.start()
-        dec_copies.append(copy)
+    barrier, callers = greet(peers)
     sent = []
 
     def send(half, along_first, step, source, target_ref, sem):
@@ -216,11 +269,15 @@
     for first in order:
         for dx, dy in sorted({(first, 2), (2, first)}):
             project(dx, dy)
+    for dx, dy in ((1, 1), (1, 3), (3, 1), (3, 3), (0, 1), (1, 0)):
+        project(dx, dy)
+    pl.semaphore_wait(barrier, callers)
+    for first in order:
         for half in (0, 1):
             send_far(half, first)
-    for dx in (1, 3, 0):
-        for dy in (1, 3, 0):
-            project(dx, dy)
+    swap_start(served_ref, landing, swap_send, swap_recv)
+    for dx, dy in ((3, 0), (0, 3), (0, 0)):
+        project(dx, dy)
     for first in order:
         for half in (0, 1):
             slot = half * SIDE + first
@@ -230,6 +287,32 @@
                 part[block, span, :] = (wide(part[block, span, :]) + wide(far[slot, quarter])).astype(jnp.bfloat16)
                 block, span = piece(half, first, step)
                 send(half, False, step, part.at[block, span], near.at[slot, quarter], near_sem.at[slot, quarter])
+    swap_finish(served_ref, landing, swap_send, swap_recv)
+    groups, item_rows, lanes = landing.shape
+    returned = landing[...].reshape(groups * item_rows, lanes).astype(jnp.bfloat16)
+    dec_att = jnp.dot(place_ref[...], returned, preferred_element_type=jnp.float32)
+    dec_att = dec_att.astype(jnp.bfloat16)[:, : w_ref.shape[0]]
+    dec_part = jnp.dot(dec_att, w_ref[...], preferred_element_type=jnp.float32)
+    dec_wide[...] = jnp.zeros(dec_wide.shape, jnp.float32)
+    per_peer = dec_part.shape[0] // 16
+    for chunk in range(dec_part.shape[1] // lanes):
+        for row in range(per_peer):
+            dec_wide[:, chunk * per_peer + row, :] = dec_part[
+                row * 16 : row * 16 + 16, chunk * lanes : (chunk + 1) * lanes
+            ]
+    dec_ref[...] = dec_wide[...].astype(jnp.bfloat16)
+    dec_copies = []
+    for k, peer in enumerate(peers):
+        copy = pltpu.make_async_remote_copy(
+            src_ref=dec_ref.at[peer],
+            dst_ref=dec_in.at[k],
+            send_sem=dec_send.at[k],
+            recv_sem=dec_recv.at[k],
+            device_id={"head": peer},
+            device_id_type=MESH,
+        )
+        copy.start()
+        dec_copies.append(copy)
     for first in order:
         for half in (0, 1):
             slot = half * SIDE + first
@@ -270,17 +353,19 @@
         copy.wait_send()
 
 
-def project_scatter(attended, weight, dec_parts):
+def project_scatter(attended, weight, served, placing):
     rows = attended.shape[0] // 16
     width = weight.shape[1]
+    lanes = served.shape[2]
+    dec_rows = -(-placing.shape[0] // 16 * width // lanes // 16) * 16
     whole = pl.BlockSpec(memory_space=pltpu.VMEM)
     return pl.pallas_call(
         functools.partial(scatter_kernel, rows),
         out_shape=(
             jax.ShapeDtypeStruct((rows, width), jnp.bfloat16),
-            jax.ShapeDtypeStruct(dec_parts.shape[1:], jnp.bfloat16),
+            jax.ShapeDtypeStruct((dec_rows, lanes), jnp.bfloat16),
         ),
-        in_specs=[whole, whole, whole],
+        in_specs=[whole, whole, whole, whole],
         out_specs=(whole, whole),
         scratch_shapes=[
             pltpu.VMEM((16, rows, width), jnp.bfloat16),
@@ -288,18 +373,23 @@
             pltpu.VMEM((8, 2, rows // 2, width), jnp.bfloat16),
             pltpu.VMEM((2, 2, rows // 4, width), jnp.bfloat16),
             pltpu.VMEM((2, 2, rows // 2, width), jnp.bfloat16),
-            pltpu.VMEM((15,) + dec_parts.shape[1:], jnp.bfloat16),
+            pltpu.VMEM(served.shape, served.dtype),
+            pltpu.VMEM((16, dec_rows, lanes), jnp.float32),
+            pltpu.VMEM((16, dec_rows, lanes), jnp.bfloat16),
+            pltpu.VMEM((15, dec_rows, lanes), jnp.bfloat16),
             pltpu.SemaphoreType.DMA((40,)),
             pltpu.SemaphoreType.DMA((10, 2)),
             pltpu.SemaphoreType.DMA((10, 2)),
             pltpu.SemaphoreType.DMA((15,)),
             pltpu.SemaphoreType.DMA((15,)),
+            pltpu.SemaphoreType.DMA((served.shape[0],)),
+            pltpu.SemaphoreType.DMA((served.shape[0],)),
         ],
         compiler_params=pltpu.CompilerParams(
             collective_id=1, has_side_effects=True, vmem_limit_bytes=40 * 2**20
         ),
         name="project_scatter",
-    )(attended, weight, dec_parts)
+    )(attended, weight, served, placing)
 
 
 def from_behind(array, axis, by):
@@ -376,7 +466,26 @@
     first_dev = lax.axis_index("head") == 0
     rim_rows = jnp.where(first_dev, stretch_tail[0], rim_rows)
     conved = convolve(rim_rows, normed, conv_taps)
-    grouped = gather_project(conved, w_flat)
+    dec_normed = rms_rows(decode_tokens[0], norm_gain).astype(jnp.bfloat16)
+    dec_conved = convolve(decode_tail[0], dec_normed[:, None, :], conv_taps)[:, 0, :]
+    dec_qkv = jnp.dot(dec_conved, w_flat, preferred_element_type=jnp.float32).astype(jnp.bfloat16)
+    owners = decode_owner[0, :, 0]
+    slots_here = decode_slot[0]
+    groups = lax.axis_size("tok")
+    capacity = max(2, 2 * DEC // groups)
+    earlier = jnp.arange(DEC)[None, :] < jnp.arange(DEC)[:, None]
+    same_owner = owners[None, :] == owners[:, None]
+    rank_in = jnp.sum(earlier & same_owner, axis=1)
+    target = owners * capacity + rank_in
+    placing = jnp.arange(groups * capacity)[:, None] == target[None, :]
+    sent_rows = jnp.dot(placing.astype(jnp.bfloat16), dec_qkv, preferred_element_type=jnp.float32)
+    sent_slots = jnp.sum(jnp.where(placing, slots_here[None, :] + 1, 0), axis=1) - 1
+    wide = head_count * block_width
+    sent = jnp.concatenate([sent_rows, sent_slots[:, None].astype(jnp.float32)], axis=1)
+    sent = sent.reshape(groups, capacity * (wide + 1))
+    lines = -(-sent.shape[1] // 1024) * 8
+    sent = jnp.pad(sent, ((0, 0), (0, lines * 128 - sent.shape[1]))).reshape(groups, lines, 128)
+    grouped, items = gather_project(conved, w_flat, sent)
     grouped = grouped.reshape(STRETCH, head_count, block_width)
     queries = grouped[:, :, :F]
     key_feats = grouped[:, :, F : 2 * F]
@@ -422,51 +531,20 @@
     state_next = state_old + jnp.einsum(
         "jhd,jhp->hdp", values, key_phi, preferred_element_type=jnp.float32
     )
-    dec_normed = rms_rows(decode_tokens[0], norm_gain).astype(jnp.bfloat16)
-    dec_conved = convolve(decode_tail[0], dec_normed[:, None, :], conv_taps)[:, 0, :]
-    dec_qkv = jnp.dot(dec_conved, w_flat, preferred_element_type=jnp.float32).astype(jnp.bfloat16)
-    owners = decode_owner[0, :, 0]
-    slots_here = decode_slot[0]
-    groups = lax.axis_size("tok")
-    capacity = max(2, 2 * DEC // groups)
-    earlier = jnp.arange(DEC)[None, :] < jnp.arange(DEC)[:, None]
-    same_owner = owners[None, :] == owners[:, None]
-    rank_in = jnp.sum(earlier & same_owner, axis=1)
-    target = owners * capacity + rank_in
-    placing = jnp.arange(groups * capacity)[:, None] == target[None, :]
-    sent_rows = jnp.dot(
-        placing.astype(jnp.bfloat16), dec_qkv, preferred_element_type=jnp.float32
-    ).astype(jnp.bfloat16)
-    sent_rows = sent_rows.reshape(groups, capacity, head_count * block_width)
-    sent_slots = jnp.sum(jnp.where(placing, slots_here[None, :] + 1, 0), axis=1) - 1
-    sent_slots = sent_slots.reshape(groups, capacity, 1).astype(jnp.bfloat16)
-    sent_rows = jnp.concatenate([sent_rows, sent_slots], axis=2)
-    item_rows = lax.all_to_all(sent_rows, "tok", split_axis=0, concat_axis=0, tiled=True)
-    item_slots = item_rows[:, :, -1].astype(jnp.int32)
-    item_rows = item_rows[:, :, :-1]
-    item_count = item_rows.shape[1]
-    flat_out = decode_items(
-        item_rows.reshape(groups * item_count, head_count * block_width),
-        item_slots.reshape(groups * item_count),
-        state_cache[0],
-        out_gain,
-        head_count,
-    )
-    served = flat_out.reshape(groups, item_count, head_count * DH)
-    returned = lax.all_to_all(served, "tok", split_axis=0, concat_axis=0, tiled=True)
-    dec_attended = jnp.dot(
-        jnp.transpose(placing).astype(jnp.bfloat16),
-        returned.reshape(groups * capacity, head_count * DH),
-        preferred_element_type=jnp.float32,
-    ).astype(jnp.bfloat16)
-    dec_part = jnp.dot(dec_attended, out_weight, preferred_element_type=jnp.float32).astype(jnp.bfloat16)
+    items = items.reshape(groups, lines * 128)[:, : capacity * (wide + 1)]
+    items = items.reshape(groups * capacity, wide + 1)
+    served = decode_items(
+        items[:, :wide], items[:, wide].astype(jnp.int32), state_cache[0], out_gain, head_count
+    )
+    served = served.astype(jnp.float32).reshape(groups, capacity, head_count * DH)
+    served = jnp.pad(served, ((0, 0), (0, 8 - capacity), (0, 128 - head_count * DH)))
     heads = lax.axis_size("head")
-    lanes = 128
-    dec_part = dec_part.reshape(heads, DEC // heads * D // lanes, lanes)
-    used = dec_part.shape[1]
-    dec_part = jnp.pad(dec_part, ((0, 0), (0, -used % 16), (0, 0)))
-    stretch_out, dec_sum = project_scatter(attended, out_weight, dec_part)
-    decode_out = dec_sum[:used].reshape(DEC // heads, D)
+    per_head = DEC // heads
+    spots = (owners * 8 + rank_in).reshape(heads, per_head).T.reshape(DEC)
+    putting = (spots[:, None] == jnp.arange(groups * 8)[None, :]).astype(jnp.bfloat16)
+    stretch_out, dec_sum = project_scatter(attended, out_weight, served, putting)
+    dec_sum = dec_sum[: per_head * D // 128].reshape(D // 128, per_head, 128)
+    decode_out = jnp.transpose(dec_sum, (1, 0, 2)).reshape(per_head, D)
     return (stretch_out[None], decode_out[None], state_next[None])
 
 

time: 129 us -> 112 us (0.87)
  starting transfers between devices: 34.5 us -> 3.93 us
  Pallas kernels: 54.7 us -> 73.3 us
  waiting for transfers between devices: 9.5 us -> 0.01 us
  local copies, waits for them, and re-layouts: 7.23 us -> 10.3 us
    all_to_all x2 -> x0, starting transfers between devices: 30.5 us -> none  [the longest x1 16.2 us: local(): lax.all_to_all(sent_rows, 'tok', split_axis=0, concat_axis=0, tiled=True)]
    pallas_call x1, Pallas kernels: 26.5 us -> 40.5 us  [gather_project(): pl.pallas_call(gather_kernel, out_shape=(jax.ShapeDtypeStruct((16 * rows,...]
    all_to_all x2 -> x0, waiting for transfers between devices: 9.49 us -> none  [the longest x1 9.49 us: local(): lax.all_to_all(served, 'tok', split_axis=0, concat_axis=0, tiled=True)]
    pallas_call x1, Pallas kernels: 28.1 us -> 32.8 us  [project_scatter(): pl.pallas_call(functools.partial(scatter_kernel, rows), out_shape=(jax.Sh...]
    dot_general x2, matrix products: 1.79 us -> 3.35 us  [local(): jnp.einsum('hij,jhd->ihd', weights, values[:finish], preferred_element_ty...]
    unnamed x22 -> x31, local copies, waits for them, and re-layouts: 2.82 us -> 3.21 us
  transfers between devices with their start and end apart: 3 -> 1, of which waited for: 1 -> 0; matrix products, arithmetic and copies ran while one was open for 15% -> 9% of each run, Pallas kernels for 21% -> 0%
where the time goes in v3:
time: 112 us
  Pallas kernels  73.3 us (65%)
  other arithmetic  11.5 us (10%)
  matrix products  10.4 us (9%)
  local copies, waits for them, and re-layouts  10.3 us (9%)
  starting transfers between devices  3.93 us (4%)
  between operations  2.39 us (2%)
    pallas_call x1, Pallas kernels, gather_project(): pl.pallas_call(gather_kernel, out_shape=(jax.ShapeDtypeStruct((16 * rows,...  40.5 us
    pallas_call x1, Pallas kernels, project_scatter(): pl.pallas_call(functools.partial(scatter_kernel, rows), out_shape=(jax.Sh...  32.8 us
    ppermute x1, starting transfers between devices, from_behind(): return lax.ppermute(array, axis, pairs)  3.93 us
    dot_general x2, matrix products, local(): jnp.einsum('hij,jhd->ihd', weights, values[:finish], preferred_element_ty...  3.35 us
    unnamed x31, local copies, waits for them, and re-layouts  3.21 us
    dot_general x1, matrix products, local(): jnp.einsum('ihp,hdp->ihd', features(queries.astype(jnp.float32)), state_o...  2.88 us
    dot_general x1, matrix products, decode_items(): jnp.einsum('nhp,shdp->nshd', features(queries), cache_own, precision=lax....  2.65 us
    reduce_sum x3, other arithmetic, rms_rows(): jnp.mean(values * values, axis=-1, keepdims=True) + 1e-05  2.35 us
  transfers between devices with their start and end apart: 1, of which 0 were waited for; matrix products, arithmetic and copies ran while one was open for 9% of the time, Pallas kernels for 0%

profile of v3, /device:TPU:1, one launch (start us, length us, event | category | flops | bytes accessed | tf_op | source)
XLA Modules:
  0.0 111.8 jit_solution(7386054826362870914)
XLA Ops:
  0.6 1.1 %fusion.37 = f32[64]{0:T(128)S(1)} fusion(bf16[1,64,1792]{2,1,0:T(8,128)(2,1)} %param.14), kind=kLoop, calls=%fused_computation.54 | loop fusion | flops 344000 | bytes 229632 | tf_op jit(solution)/shard_map/reduce_sum | solution.py:403
  1.8 1.1 fusion.39
  2.9 3.9 %collective-permute-start = (bf16[2,1792]{1,0:T(2,128)(2,1)S(1)}, bf16[2,1792]{1,0:T(2,128)(2,1)S(1)}, u32[]{:S(2)}, u32[]{:S(2)}) collective-permute-start(bf16[2,1792]{1,0:T(2,128)(2,1)S(1)} %slice.116), channel_id=1, source_target_pairs={{0,32},{32,64},{64,96},{96,128},{128,160},{160,192},{192,224},{224... | collective-permute-start | bytes 21512 | tf_op jit(solution)/shard_map/ppermute | solution.py:398
  6.8 0.7 multiply_reduce_fusion.2
  7.5 0.9 convert_reduce_fusion
  8.4 0.7 multiply_add_fusion.1
  10.5 0.7 add_bitcast_fusion.1
  11.2 1.0 fusion.49
  12.6 0.9 slice_reduce_fusion.2
  13.6 1.0 fusion.48
  14.6 1.0 copy.119
  15.7 0.4 fusion.12
  16.3 0.9 constant_dynamic-slice_fusion
  17.6 0.6 slice.106
  18.8 40.5 %gather_project.1 = (bf16[1024,144]{1,0:T(8,128)(2,1)S(1)}, f32[32,8,128]{2,1,0:T(8,128)S(1)}) custom-call(bf16[64,1792]{1,0:T(8,128)(2,1)S(1)} %fusion.41.own_ref, bf16[1792,144]{1,0:T(8,128)(2,1)S(1)} %bitcast.138, f32[32,8,128]{2,1,0:T(8,128)S(1)} %bitcast.144), custom_call_target="tpu_custom_call" | custom-call | tf_op jit(solution)/shard_map/gather_project/pallas_call | solution.py:193
  59.6 0.8 convert_multiply_fusion.1
  60.5 1.0 fusion.25
  61.8 0.6 multiply_add_fusion
  62.4 0.7 copy.82
  63.2 2.6 %fusion.6 = f32[512,1,112]{2,0,1:T(8,128)} fusion(s32[512]{0:T(512)} %slice.106, pred[1024]{0:T(1024)(128)(4,1)} %copy-done.10, bf16[1024,1,144]{2,0,1:T(8,128)(2,1)S(1)} %bitcast.141), kind=kOutput, calls=%fused_computation.10 | convolution fusion | flops 138936320 | bytes 887808 | tf_op jit(solution)/shard_map/hij,jhd->ihd/dot_general | solution.py:519
  65.8 2.7 %fusion = f32[64,16,112]{2,0,1:T(8,128)S(1)} fusion(f32[1,16,1,112,273]{3,2,4,1,0:T(1,128)S(1)} %copy-done.1, f32[64,1,256]{2,0,1:T(8,128)} %copy.82, f32[64,1,16]{2,0,1:T(8,128)S(1)} %get-tuple-element.31, f32[273]{0:T(512)S(1)} %pad.21.clone), kind=kOutput, calls=%fused_computation | convolution fusion | flops 375752832 | bytes 2486340 | tf_op jit(solution)/shard_map/nhp,shdp->nshd/dot_general | solution.py:432
  68.5 0.7 fusion.26
  69.5 1.2 %copy.76 = f32[1024,1,16]{0,2,1:T(8,128)S(1)} copy(f32[1024,1,16]{2,0,1:T(8,128)} %convert_multiply_fusion.1) | data formatting | bytes 131072 | tf_op jit(solution)/shard_map/div | solution.py:409
  70.7 1.1 copy.89
  72.3 0.4 fusion.11
  72.7 0.8 copy.90
  73.6 0.7 convolution_bitcast_fusion.1
  74.4 2.9 %multiply_reduce_fusion = (f32[1024]{0:T(1024)S(1)}, f32[1024,1,112]{2,0,1:T(8,128)S(1)}) fusion(f32[512,1,112]{2,0,1:T(8,128)S(1)} %copy-done.4, f32[512,1,112]{2,0,1:T(8,128)S(1)} %convolution_bitcast_fusion.1, f32[1024,1,256]{0,2,1:T(8,128)S(1)} %bitcast.148, f32[1024,1,16]{0,2,1:T(8,128)S(1)} %copy.76, f32[273]{0:T(512)S(1)} %pad.21.clone, ...), kind=kOutput, calls=%fused_computation.45 | convolution fusion | flops 376734720 | bytes 2159108 | tf_op jit(solution)/shard_map/ihp,hdp->ihd/dot_general | solution.py:497
  77.3 0.3 fusion.43.att_ref
  77.7 32.8 %project_scatter.1 = (bf16[64,1792]{1,0:T(8,128)(2,1)S(1)}, bf16[32,128]{1,0:T(8,128)(2,1)S(1)}) custom-call(bf16[1024,112]{1,0:T(8,128)(2,1)S(1)} %fusion.43.att_ref, bf16[112,1792]{1,0:T(8,128)(2,1)S(1)} %copy-done, f32[32,8,128]{2,1,0:T(8,128)S(1)} %pad_convert_fusion.served_ref, bf16[32,256]{1,0:T(8,128)(2,1)S(1)} %fusion.75.place_ref), custom_call_target="tpu_custom_call" | custom-call | tf_op jit(solution)/shard_map/project_scatter/pallas_call | solution.py:362
  110.5 0.6 broadcast_in_dim_reshape.2
  111.1 0.7 copy.126
  (74 shorter events, 3.3 us)
Async XLA Ops:
  0.6 15.1 %copy-start.3 = (bf16[1792,1,144]{0,2,1:T(8,128)(2,1)S(1)}, bf16[1792,1,144]{0,2,1:T(8,128)(2,1)}, u32[]{:S(2)}) copy-start(bf16[1792,1,144]{0,2,1:T(8,128)(2,1)} %param.20) | copy-start | bytes 1548292
  2.9 15.3 %collective-permute-start = (bf16[2,1792]{1,0:T(2,128)(2,1)S(1)}, bf16[2,1792]{1,0:T(2,128)(2,1)S(1)}, u32[]{:S(2)}, u32[]{:S(2)}) collective-permute-start(bf16[2,1792]{1,0:T(2,128)(2,1)S(1)} %slice.116), channel_id=1, source_target_pairs={{0,32},{32,64},{64,96},{96,128},{128,160},{160,192},{192,224},{224... | collective-permute-start | bytes 21512 | tf_op jit(solution)/shard_map/ppermute | solution.py:398
  15.6 2.6 %copy-start.6 = (bf16[1,2,1792]{2,1,0:T(2,128)(2,1)S(1)}, bf16[1,2,1792]{2,1,0:T(2,128)(2,1)}, u32[]{:S(2)}) copy-start(bf16[1,2,1792]{2,1,0:T(2,128)(2,1)} %param.15) | copy-start | bytes 21508
  17.3 42.0 %copy-start.10 = (pred[1024]{0:T(1024)(128)(4,1)}, pred[1024]{0:T(1024)(128)(4,1)S(1)}, u32[]{:S(2)}) copy-start(pred[1024]{0:T(1024)(128)(4,1)S(1)} %iota_compare_fusion.6) | copy-start | bytes 3076
  18.2 0.6 copy-start.5
  63.2 2.7 %copy-start.1 = (f32[1,16,1,112,273]{3,2,4,1,0:T(1,128)S(1)}, f32[1,16,1,112,273]{3,2,4,1,0:T(1,128)}, u32[]{:S(2)}) copy-start(f32[1,16,1,112,273]{3,2,4,1,0:T(1,128)} %param.23) | copy-start | bytes 5870596
  65.8 3.4 %copy-start.7 = (f32[64]{0:T(128)S(1)}, f32[64]{0:T(128)}, u32[]{:S(2)}) copy-start(f32[64]{0:T(128)} %multiply_add_fusion) | copy-start | bytes 772
  65.8 3.6 %copy-start.8 = (f32[112]{0:T(128)S(1)}, f32[112]{0:T(128)}, u32[]{:S(2)}) copy-start(f32[112]{0:T(128)} %param.21) | copy-start | bytes 1348
  68.5 3.3 %copy-start.2 = (f32[1024,16]{1,0:T(8,128)S(1)}, f32[1024,16]{1,0:T(8,128)}, u32[]{:S(2)}) copy-start(f32[1024,16]{1,0:T(8,128)} %get-tuple-element.27) | copy-start | bytes 196612
  68.5 3.8 %copy-start.11 = (pred[1024]{0:T(1024)(128)(4,1)S(1)}, pred[1024]{0:T(1024)(128)(4,1)}, u32[]{:S(2)}) copy-start(pred[1024]{0:T(1024)(128)(4,1)} %copy-done.10) | copy-start | bytes 3076
  72.1 1.5 %slice-start = ((s32[1024]{0:T(1024)}), s32[512]{0:T(512)S(1)}, s32[]{:S(2)}) async-start(s32[1024]{0:T(1024)} %copy-done.5), calls=%async_computation | async-start | bytes 4096 | tf_op jit(solution)/shard_map/slice | solution.py:514
  72.1 1.5 %slice-start.1 = ((pred[1024]{0:T(1024)(128)(4,1)}), pred[512]{0:T(512)(128)(4,1)S(1)}, s32[]{:S(2)}) async-start(pred[1024]{0:T(1024)(128)(4,1)} %copy-done.10), calls=%async_computation.1 | async-start | bytes 1024 | tf_op jit(solution)/shard_map/slice | solution.py:514
  73.5 0.9 copy-start.4
  73.6 3.7 %copy-start.9 = (f32[112]{0:T(128)S(1)}, f32[112]{0:T(128)}, u32[]{:S(2)}) copy-start(f32[112]{0:T(128)} %param.21) | copy-start | bytes 1348
  74.4 3.3 %copy-start = (bf16[112,1792]{1,0:T(8,128)(2,1)S(1)}, bf16[112,1792]{1,0:T(8,128)(2,1)}, u32[]{:S(2)}) copy-start(bf16[112,1792]{1,0:T(8,128)(2,1)} %w_ref.1) | copy-start | bytes 1204228

commit v4 on v3

--- a/solution.py
+++ b/solution.py
@@ -94,7 +94,8 @@
 
 
 def gather_kernel(
-    own_ref, w_ref, items_ref, qkv_ref, got_ref, buf, landing, send_sem, recv_sem, swap_send, swap_recv
+    own_ref, w_ref, tokens_ref, tails_ref, gain_ref, taps_ref, put_ref, slot_ref, qkv_ref, got_ref,
+    buf, items_ref, landing, send_sem, recv_sem, swap_send, swap_recv,
 ):
     me, mx, my = plane_position()
     rows = own_ref.shape[0]
@@ -137,6 +138,15 @@
         product = jnp.dot(value, w_ref[...], preferred_element_type=jnp.float32)
         qkv_ref[pl.ds(pl.multiple_of(block * rows, rows), rows), :] = product.astype(jnp.bfloat16)
 
+    normed = rms_rows(tokens_ref[...], gain_ref[...]).astype(jnp.bfloat16).astype(jnp.float32)
+    width = own_ref.shape[1]
+    total = taps_ref[0:1, :] * tails_ref[:, :width].astype(jnp.float32)
+    total = total + taps_ref[1:2, :] * tails_ref[:, width:].astype(jnp.float32)
+    total = (total + taps_ref[2:3, :] * normed).astype(jnp.bfloat16)
+    dec_qkv = jnp.dot(total, w_ref[...], preferred_element_type=jnp.float32).astype(jnp.bfloat16)
+    placed = jnp.dot(put_ref[...], dec_qkv, preferred_element_type=jnp.float32) + slot_ref[...]
+    items_ref[...] = jnp.zeros(items_ref.shape, jnp.float32)
+    items_ref[:, :, : w_ref.shape[1]] = placed.reshape(items_ref.shape[:2] + (w_ref.shape[1],))
     project(me, own_ref[...])
     pl.semaphore_wait(barrier, callers)
     for along_first in (False, True):
@@ -186,31 +196,33 @@
         copy.wait_send()
 
 
-def gather_project(conved, weight, items):
+def gather_project(conved, weight, tokens, tails, gain, taps, putting, slots):
     rows, width = conved.shape
     columns = weight.shape[1]
+    swapped = (putting.shape[0] // 8, 8, -(-columns // 128) * 128)
     whole = pl.BlockSpec(memory_space=pltpu.VMEM)
     return pl.pallas_call(
         gather_kernel,
         out_shape=(
             jax.ShapeDtypeStruct((16 * rows, columns), jnp.bfloat16),
-            jax.ShapeDtypeStruct(items.shape, items.dtype),
+            jax.ShapeDtypeStruct(swapped, jnp.float32),
         ),
-        in_specs=[whole, whole, whole],
+        in_specs=[whole] * 8,
         out_specs=(whole, whole),
         scratch_shapes=[
             pltpu.VMEM((16, rows, width), jnp.bfloat16),
-            pltpu.VMEM(items.shape, items.dtype),
+            pltpu.VMEM(swapped, jnp.float32),
+            pltpu.VMEM(swapped, jnp.float32),
             pltpu.SemaphoreType.DMA((40,)),
             pltpu.SemaphoreType.DMA((32, 2)),
-            pltpu.SemaphoreType.DMA((items.shape[0],)),
-            pltpu.SemaphoreType.DMA((items.shape[0],)),
+            pltpu.SemaphoreType.DMA((swapped[0],)),
+            pltpu.SemaphoreType.DMA((swapped[0],)),
         ],
         compiler_params=pltpu.CompilerParams(
             collective_id=0, has_side_effects=True, vmem_limit_bytes=40 * 2**20
         ),
         name="gather_project",
-    )(conved, weight, items)
+    )(conved, weight, tokens, tails, gain, taps, putting, slots)
 
 
 def scatter_kernel(
@@ -407,8 +419,15 @@
 def features(vectors):
     breadth = vectors.shape[-1]
     linear = vectors / math.sqrt(math.sqrt(breadth))
-    outer = vectors[..., :, None] * vectors[..., None, :] / math.sqrt(2.0 * breadth)
-    outer = outer.reshape(vectors.shape[:-1] + (breadth * breadth,))
+    index = jnp.arange(breadth * breadth)[None, :]
+    which = jnp.arange(breadth)[:, None]
+    slow = (index // breadth == which).astype(jnp.bfloat16)
+    fast = (index % breadth == which).astype(jnp.bfloat16)
+    exact = vectors.astype(jnp.bfloat16)
+    outer = jnp.dot(exact, slow, preferred_element_type=jnp.float32) * jnp.dot(
+        exact, fast, preferred_element_type=jnp.float32
+    )
+    outer = outer / math.sqrt(2.0 * breadth)
     ones = jnp.ones(vectors.shape[:-1] + (1,), vectors.dtype)
     return jnp.concatenate([ones, linear, outer], axis=-1)
 
@@ -466,9 +485,6 @@
     first_dev = lax.axis_index("head") == 0
     rim_rows = jnp.where(first_dev, stretch_tail[0], rim_rows)
     conved = convolve(rim_rows, normed, conv_taps)
-    dec_normed = rms_rows(decode_tokens[0], norm_gain).astype(jnp.bfloat16)
-    dec_conved = convolve(decode_tail[0], dec_normed[:, None, :], conv_taps)[:, 0, :]
-    dec_qkv = jnp.dot(dec_conved, w_flat, preferred_element_type=jnp.float32).astype(jnp.bfloat16)
     owners = decode_owner[0, :, 0]
     slots_here = decode_slot[0]
     groups = lax.axis_size("tok")
@@ -476,16 +492,15 @@
     earlier = jnp.arange(DEC)[None, :] < jnp.arange(DEC)[:, None]
     same_owner = owners[None, :] == owners[:, None]
     rank_in = jnp.sum(earlier & same_owner, axis=1)
-    target = owners * capacity + rank_in
-    placing = jnp.arange(groups * capacity)[:, None] == target[None, :]
-    sent_rows = jnp.dot(placing.astype(jnp.bfloat16), dec_qkv, preferred_element_type=jnp.float32)
-    sent_slots = jnp.sum(jnp.where(placing, slots_here[None, :] + 1, 0), axis=1) - 1
-    wide = head_count * block_width
-    sent = jnp.concatenate([sent_rows, sent_slots[:, None].astype(jnp.float32)], axis=1)
-    sent = sent.reshape(groups, capacity * (wide + 1))
-    lines = -(-sent.shape[1] // 1024) * 8
-    sent = jnp.pad(sent, ((0, 0), (0, lines * 128 - sent.shape[1]))).reshape(groups, lines, 128)
-    grouped, items = gather_project(conved, w_flat, sent)
+    spots = owners * 8 + rank_in
+    lines = jnp.arange(groups * 8)
+    gathering = (lines[:, None] == spots[None, :]).astype(jnp.bfloat16)
+    named = lines[:, None] == spots[None, :] + capacity
+    slot_column = jnp.sum(jnp.where(named, slots_here[None, :], 0), axis=1, keepdims=True)
+    grouped, items = gather_project(
+        conved, w_flat, decode_tokens[0], decode_tail[0].reshape(DEC, 2 * D), norm_gain[None],
+        conv_taps, gathering, slot_column.astype(jnp.float32),
+    )
     grouped = grouped.reshape(STRETCH, head_count, block_width)
     queries = grouped[:, :, :F]
     key_feats = grouped[:, :, F : 2 * F]
@@ -531,17 +546,18 @@
     state_next = state_old + jnp.einsum(
         "jhd,jhp->hdp", values, key_phi, preferred_element_type=jnp.float32
     )
-    items = items.reshape(groups, lines * 128)[:, : capacity * (wide + 1)]
-    items = items.reshape(groups * capacity, wide + 1)
+    wide = head_count * block_width
+    item_rows = items[:, :capacity, :wide].reshape(groups * capacity, wide)
+    item_slots = items[:, capacity : 2 * capacity, 0].reshape(groups * capacity)
     served = decode_items(
-        items[:, :wide], items[:, wide].astype(jnp.int32), state_cache[0], out_gain, head_count
+        item_rows, item_slots.astype(jnp.int32), state_cache[0], out_gain, head_count
     )
     served = served.astype(jnp.float32).reshape(groups, capacity, head_count * DH)
     served = jnp.pad(served, ((0, 0), (0, 8 - capacity), (0, 128 - head_count * DH)))
     heads = lax.axis_size("head")
     per_head = DEC // heads
-    spots = (owners * 8 + rank_in).reshape(heads, per_head).T.reshape(DEC)
-    putting = (spots[:, None] == jnp.arange(groups * 8)[None, :]).astype(jnp.bfloat16)
+    returns = spots.reshape(heads, per_head).T.reshape(DEC)
+    putting = (returns[:, None] == jnp.arange(groups * 8)[None, :]).astype(jnp.bfloat16)
     stretch_out, dec_sum = project_scatter(attended, out_weight, served, putting)
     dec_sum = dec_sum[: per_head * D // 128].reshape(D // 128, per_head, 128)
     decode_out = jnp.transpose(dec_sum, (1, 0, 2)).reshape(per_head, D)

time: 112 us -> 111 us (level)
  matrix products: 10.4 us -> 13.4 us
  local copies, waits for them, and re-layouts: 10.3 us -> 8.04 us
  other arithmetic: 11.5 us -> 9.25 us
    dot_general x1 -> x6, matrix products: 0.44 us -> 3.47 us  [the longest x3 1.89 us: features(): jnp.dot(exact, fast, preferred_element_type=jnp.float32)]
    reduce_sum x3 -> x2, other arithmetic: 2.35 us -> 1.3 us  [rms_rows(): jnp.mean(values * values, axis=-1, keepdims=True) + 1e-05]
    unnamed x31 -> x34, local copies, waits for them, and re-layouts: 3.21 us -> 3.36 us
  transfers between devices with their start and end apart: 1 -> 1, of which waited for: 0 -> 0; matrix products, arithmetic and copies ran while one was open for 9% -> 7% of each run, Pallas kernels for 0% -> 0%
where the time goes in v4:
time: 111 us; the launch traced here: 110 us
  Pallas kernels  73.3 us (66%)
  matrix products  13.4 us (12%)
  other arithmetic  9.25 us (8%)
  local copies, waits for them, and re-layouts  8.04 us (7%)
  starting transfers between devices  3.93 us (4%)
  between operations  2.39 us (2%)
    pallas_call x1, Pallas kernels, gather_project(): pl.pallas_call(gather_kernel, out_shape=(jax.ShapeDtypeStruct((16 * rows,...  40.5 us
    pallas_call x1, Pallas kernels, project_scatter(): pl.pallas_call(functools.partial(scatter_kernel, rows), out_shape=(jax.Sh...  32.8 us
    ppermute x1, starting transfers between devices, from_behind(): return lax.ppermute(array, axis, pairs)  3.93 us
    dot_general x1, matrix products, decode_items(): jnp.einsum('nhp,shdp->nshd', features(queries), cache_own, precision=lax....  3.43 us
    unnamed x34, local copies, waits for them, and re-layouts  3.36 us
    dot_general x1, matrix products, local(): jnp.einsum('ihp,hdp->ihd', features(queries.astype(jnp.float32)), state_o...  2.88 us
    dot_general x2, matrix products, local(): jnp.einsum('hij,jhd->ihd', weights, values[:finish], preferred_element_ty...  2.52 us
  transfers between devices with their start and end apart: 1, of which 0 were waited for; matrix products, arithmetic and copies ran while one was open for 7% of the time, Pallas kernels for 0%

profile of v4, /device:TPU:1, one launch (start us, length us, event | category | flops | bytes accessed | tf_op | source)
XLA Modules:
  0.0 110.3 jit_solution(4610822714096020755)
XLA Ops:
  0.7 1.1 %fusion.39 = f32[64]{0:T(128)S(1)} fusion(bf16[1,64,1792]{2,1,0:T(8,128)(2,1)} %param.14), kind=kLoop, calls=%fused_computation.55 | loop fusion | flops 344000 | bytes 229632 | tf_op jit(solution)/shard_map/reduce_sum | solution.py:415
  1.8 1.1 fusion.41
  2.9 3.9 %collective-permute-start = (bf16[2,1792]{1,0:T(2,128)(2,1)S(1)}, bf16[2,1792]{1,0:T(2,128)(2,1)S(1)}, u32[]{:S(2)}, u32[]{:S(2)}) collective-permute-start(bf16[2,1792]{1,0:T(2,128)(2,1)S(1)} %slice.97), channel_id=1, source_target_pairs={{0,32},{32,64},{64,96},{96,128},{128,160},{160,192},{192,224},{224... | collective-permute-start | bytes 21512 | tf_op jit(solution)/shard_map/ppermute | solution.py:410
  6.9 0.9 convert_reduce_fusion.1
  7.8 0.7 broadcast_add_fusion
  8.5 0.7 multiply_reduce_fusion.2
  9.2 0.9 slice_reduce_fusion.2
  11.8 0.8 select_reduce_fusion
  12.5 0.9 constant_dynamic-slice_fusion
  13.5 0.7 broadcast_in_dim.57.gain_ref
  14.4 1.4 %copy.49 = bf16[1792,1,144]{2,0,1:T(8,128)(2,1)S(1)} copy(bf16[1792,1,144]{0,2,1:T(8,128)(2,1)} %param.20) | data formatting | bytes 1032192 | tf_op args[6]
  15.8 0.6 slice.88
  16.7 40.5 %gather_project.1 = (bf16[1024,144]{1,0:T(8,128)(2,1)S(1)}, f32[32,8,256]{2,1,0:T(8,128)S(1)}) custom-call(bf16[64,1792]{1,0:T(8,128)(2,1)S(1)} %fusion.43.own_ref, bf16[1792,144]{1,0:T(8,128)(2,1)S(1)} %bitcast.132, bf16[32,1792]{1,0:T(8,128)(2,1)S(1)} %bitcast.135, bf16[32,3584]{1,0:T(8,128)(2,1)S(1)} %bitcast.133, ...), custom_call_target="tpu_custom_call" | custom-call | tf_op jit(solution)/shard_map/gather_project/pallas_call | solution.py:204
  57.2 1.2 %convert_reduce_fusion = s32[32,2]{1,0:T(8,128)} fusion(f32[32,8,256]{2,1,0:T(8,128)S(1)} %get-tuple-element.8), kind=kLoop, calls=%fused_computation.102 | loop fusion | flops 64 | bytes 512 | tf_op jit(solution)/shard_map/convert_element_type | solution.py:553
  58.8 0.3 fusion.52
  59.2 1.1 %fusion.47 = f32[1024,256]{0,1:T(8,128)S(1)} fusion(bf16[1024,1,144]{2,0,1:T(8,128)(2,1)S(1)} %bitcast.125, s32[256]{0:T(256)} %copy-done.9), kind=kOutput, calls=%fused_computation.67 | convolution fusion | flops 8392704 | bytes 1311744 | tf_op jit(solution)/shard_map/dot_general | solution.py:427
  60.3 0.9 multiply_bitcast_fusion
  61.5 3.4 %fusion = f32[64,16,112]{2,0,1:T(8,128)S(1)} fusion(f32[1,16,1,112,273]{3,2,4,1,0:T(1,128)} %param.23, f32[64,1,256]{2,0,1:T(8,128)S(1)} %fusion.17, f32[64,1,16]{2,0,1:T(8,128)S(1)} %get-tuple-element.29, f32[273]{0:T(512)S(1)} %pad.16.clone), kind=kOutput, calls=%fused_computation | convolution fusion | flops 375752832 | bytes 2486340 | tf_op jit(solution)/shard_map/nhp,shdp->nshd/dot_general | solution.py:451
  65.0 0.7 fusion.30
  65.9 0.8 multiply_convert_fusion
  66.7 1.3 %fusion.5 = f32[1024,1,256]{0,2,1:T(8,128)} fusion(f32[1024,256]{0,1:T(8,128)S(1)} %fusion.52, bf16[1024,1,144]{2,0,1:T(8,128)(2,1)S(1)} %bitcast.127, s32[256]{0:T(256)S(1)} %and_select_fusion), kind=kOutput, calls=%fused_computation.9 | convolution fusion | flops 8916992 | bytes 2360320 | tf_op jit(solution)/shard_map/dot_general | solution.py:427
  68.0 1.8 %fusion.10 = f32[512,1,112]{2,0,1:T(8,128)} fusion(s32[512]{0:T(512)S(1)} %copy-done.11, pred[1024]{0:T(1024)(128)(4,1)S(1)} %copy-done.14, bf16[1024,1,144]{2,0,1:T(8,128)(2,1)S(1)} %bitcast.128), kind=kOutput, calls=%fused_computation.16 | convolution fusion | flops 138936320 | bytes 887808 | tf_op jit(solution)/shard_map/hij,jhd->ihd/dot_general | solution.py:534
  70.0 0.7 convolution_bitcast_fusion.1
  70.7 0.3 copy-done.3
  71.1 2.9 %multiply_reduce_fusion = (f32[1024]{0:T(1024)S(1)}, f32[1024,1,112]{2,0,1:T(8,128)S(1)}) fusion(f32[512,1,112]{2,0,1:T(8,128)S(1)} %copy-done.5, f32[512,1,112]{2,0,1:T(8,128)S(1)} %convolution_bitcast_fusion.1, f32[1024,1,256]{0,2,1:T(8,128)S(1)} %copy-done.3, f32[1024,1,16]{0,2,1:T(8,128)S(1)} %copy.51, f32[273]{0:T(512)S(1)} %pad.16.clone, ...), kind=kOutput, calls=%fused_computation.46 | convolution fusion | flops 376734720 | bytes 2159108 | tf_op jit(solution)/shard_map/ihp,hdp->ihd/dot_general | solution.py:512
  74.0 0.3 fusion.45.att_ref
  74.4 32.8 %project_scatter.1 = (bf16[64,1792]{1,0:T(8,128)(2,1)S(1)}, bf16[32,128]{1,0:T(8,128)(2,1)S(1)}) custom-call(bf16[1024,112]{1,0:T(8,128)(2,1)S(1)} %fusion.45.att_ref, bf16[112,1792]{1,0:T(8,128)(2,1)S(1)} %copy-done, f32[32,8,128]{2,1,0:T(8,128)S(1)} %pad_convert_fusion.served_ref, bf16[32,256]{1,0:T(8,128)(2,1)S(1)} %fusion.71.place_ref), custom_call_target="tpu_custom_call" | custom-call | tf_op jit(solution)/shard_map/project_scatter/pallas_call | solution.py:374
  107.2 0.6 broadcast_in_dim_reshape.2
  107.8 0.4 fusion.7
  108.4 0.4 fusion.15
  108.8 0.8 copy.60
  109.6 0.7 copy.91
  (72 shorter events, 2.2 us)
Async XLA Ops:
  0.6 15.1 %copy-start.6 = (bf16[1,32,2,1792]{3,2,1,0:T(2,128)(2,1)S(1)}, bf16[1,32,2,1792]{3,2,1,0:T(2,128)(2,1)}, u32[]{:S(2)}) copy-start(bf16[1,32,2,1792]{3,2,1,0:T(2,128)(2,1)} %param.17) | copy-start | bytes 688132
  0.6 15.8 %copy-start.10 = (bf16[1,2,1792]{2,1,0:T(2,128)(2,1)S(1)}, bf16[1,2,1792]{2,1,0:T(2,128)(2,1)}, u32[]{:S(2)}) copy-start(bf16[1,2,1792]{2,1,0:T(2,128)(2,1)} %param.15) | copy-start | bytes 21508
  2.9 13.5 %collective-permute-start = (bf16[2,1792]{1,0:T(2,128)(2,1)S(1)}, bf16[2,1792]{1,0:T(2,128)(2,1)S(1)}, u32[]{:S(2)}, u32[]{:S(2)}) collective-permute-start(bf16[2,1792]{1,0:T(2,128)(2,1)S(1)} %slice.97), channel_id=1, source_target_pairs={{0,32},{32,64},{64,96},{96,128},{128,160},{160,192},{192,224},{224... | collective-permute-start | bytes 21512 | tf_op jit(solution)/shard_map/ppermute | solution.py:410
  6.8 52.0 %copy-start.9 = (s32[256]{0:T(256)}, s32[256]{0:T(256)S(1)}, u32[]{:S(2)}) copy-start(s32[256]{0:T(256)S(1)} %and_select_fusion.1) | copy-start | bytes 3076
  13.5 3.2 %copy-start.13 = (pred[1024]{0:T(1024)(128)(4,1)}, pred[1024]{0:T(1024)(128)(4,1)S(1)}, u32[]{:S(2)}) copy-start(pred[1024]{0:T(1024)(128)(4,1)S(1)} %iota_compare_fusion.14) | copy-start | bytes 3076
  14.3 2.3 %copy-start.1 = (bf16[1,32,1792]{2,1,0:T(8,128)(2,1)S(1)}, bf16[1,32,1792]{2,1,0:T(8,128)(2,1)}, u32[]{:S(2)}) copy-start(bf16[1,32,1792]{2,1,0:T(8,128)(2,1)} %param.16) | copy-start | bytes 344068
  14.4 2.3 %copy-start.2 = (f32[3,1792]{1,0:T(4,128)S(1)}, f32[3,1792]{1,0:T(4,128)}, u32[]{:S(2)}) copy-start(f32[3,1792]{1,0:T(4,128)} %taps_ref.1) | copy-start | bytes 64516
  15.8 41.4 %copy-start.8 = (s32[1024]{0:T(1024)}, s32[1024]{0:T(1024)S(1)}, u32[]{:S(2)}) copy-start(s32[1024]{0:T(1024)S(1)} %iota.59) | copy-start | bytes 12292
  58.5 2.7 %copy-start.7 = (s32[32,2]{1,0:T(8,128)S(1)}, s32[32,2]{1,0:T(8,128)}, u32[]{:S(2)}) copy-start(s32[32,2]{1,0:T(8,128)} %convert_reduce_fusion) | copy-start | bytes 772
  65.0 3.0 %copy-start.11 = (s32[512]{0:T(512)S(1)}, s32[512]{0:T(512)}, u32[]{:S(2)}) copy-start(s32[512]{0:T(512)} %slice.88) | copy-start | bytes 6148
  65.0 3.0 %copy-start.14 = (pred[1024]{0:T(1024)(128)(4,1)S(1)}, pred[1024]{0:T(1024)(128)(4,1)}, u32[]{:S(2)}) copy-start(pred[1024]{0:T(1024)(128)(4,1)} %copy-done.13) | copy-start | bytes 3076
  68.0 2.0 %slice-start = ((s32[1024]{0:T(1024)}), s32[512]{0:T(512)S(1)}, s32[]{:S(2)}) async-start(s32[1024]{0:T(1024)} %copy-done.8), calls=%async_computation | async-start | bytes 4096 | tf_op jit(solution)/shard_map/slice | solution.py:529
  68.0 2.0 %slice-start.1 = ((pred[1024]{0:T(1024)(128)(4,1)}), pred[512]{0:T(512)(128)(4,1)S(1)}, s32[]{:S(2)}) async-start(pred[1024]{0:T(1024)(128)(4,1)} %copy-done.13), calls=%async_computation.1 | async-start | bytes 1024 | tf_op jit(solution)/shard_map/slice | solution.py:529
  69.8 1.2 %copy-start.3 = (f32[1024,1,256]{0,2,1:T(8,128)S(1)}, f32[1024,1,256]{0,2,1:T(8,128)}, u32[]{:S(2)}) copy-start(f32[1024,1,256]{0,2,1:T(8,128)} %fusion.5) | copy-start | bytes 3145732
  70.0 1.1 %copy-start.5 = (f32[512,1,112]{2,0,1:T(8,128)S(1)}, f32[512,1,112]{2,0,1:T(8,128)}, u32[]{:S(2)}) copy-start(f32[512,1,112]{2,0,1:T(8,128)} %fusion.10) | copy-start | bytes 688132
  70.0 4.0 %copy-start.12 = (f32[112]{0:T(128)S(1)}, f32[112]{0:T(128)}, u32[]{:S(2)}) copy-start(f32[112]{0:T(128)} %param.21) | copy-start | bytes 1348
  71.1 3.3 %copy-start = (bf16[112,1792]{1,0:T(8,128)(2,1)S(1)}, bf16[112,1792]{1,0:T(8,128)(2,1)}, u32[]{:S(2)}) copy-start(bf16[112,1792]{1,0:T(8,128)(2,1)} %w_ref.1) | copy-start | bytes 1204228
  74.0 34.2 %copy-start.4 = (bf16[1024,1,1,1,1,1,16]{6,0,5,4,3,2,1:T(8,128)(2,1)S(1)}, bf16[1024,1,1,1,1,1,16]{6,0,5,4,3,2,1:T(8,128)(2,1)}, u32[]{:S(2)}) copy-start(bf16[1024,1,1,1,1,1,16]{6,0,5,4,3,2,1:T(8,128)(2,1)} %multiply_bitcast_fusion) | copy-start | bytes 98308

commit v5 on v4

--- a/solution.py
+++ b/solution.py
@@ -138,7 +138,7 @@
         product = jnp.dot(value, w_ref[...], preferred_element_type=jnp.float32)
         qkv_ref[pl.ds(pl.multiple_of(block * rows, rows), rows), :] = product.astype(jnp.bfloat16)
 
-    normed = rms_rows(tokens_ref[...], gain_ref[...]).astype(jnp.bfloat16).astype(jnp.float32)
+    normed = rms_rows(tokens_ref[...], gain_ref[...][None, :]).astype(jnp.bfloat16).astype(jnp.float32)
     width = own_ref.shape[1]
     total = taps_ref[0:1, :] * tails_ref[:, :width].astype(jnp.float32)
     total = total + taps_ref[1:2, :] * tails_ref[:, width:].astype(jnp.float32)
@@ -449,7 +449,7 @@
     values = shaped[:, :, 2 * F :]
     slot_total = cache_own.shape[0]
     table = jnp.einsum(
-        "nhp,shdp->nshd", features(queries), cache_own, precision=lax.Precision.HIGHEST
+        "nhp,shdp->nshd", features(queries), cache_own, precision=lax.Precision.HIGH
     )
     picker = (slot_items[:, None] == jnp.arange(slot_total)[None, :]).astype(jnp.float32)
     carried = jnp.einsum("ns,nshd->nhd", picker, table, precision=lax.Precision.HIGHEST)
@@ -498,7 +498,7 @@
     named = lines[:, None] == spots[None, :] + capacity
     slot_column = jnp.sum(jnp.where(named, slots_here[None, :], 0), axis=1, keepdims=True)
     grouped, items = gather_project(
-        conved, w_flat, decode_tokens[0], decode_tail[0].reshape(DEC, 2 * D), norm_gain[None],
+        conved, w_flat, decode_tokens[0], decode_tail[0].reshape(DEC, 2 * D), norm_gain,
         conv_taps, gathering, slot_column.astype(jnp.float32),
     )
     grouped = grouped.reshape(STRETCH, head_count, block_width)
@@ -513,7 +513,7 @@
         "ihp,hdp->ihd",
         features(queries.astype(jnp.float32)),
         state_old,
-        precision=lax.Precision.HIGHEST,
+        precision=lax.Precision.HIGH,
     )
     block_rows = min(512, STRETCH)
     pieces = []

time: 111 us -> 108 us (0.973)
  matrix products: 13.4 us -> 11.4 us
    dot_general x1, matrix products: 2.88 us -> 1.6 us  [local(): jnp.einsum('ihp,hdp->ihd', features(queries.astype(jnp.float32)), state_o...]
    unnamed x34 -> x36, local copies, waits for them, and re-layouts: 3.36 us -> 3.38 us
where the time goes in v5:
time: 108 us
  Pallas kernels  73.3 us (68%)
  matrix products  11.4 us (11%)
  other arithmetic  9.26 us (9%)
  local copies, waits for them, and re-layouts  7.36 us (7%)
  starting transfers between devices  3.93 us (4%)
  between operations  2.41 us (2%)
    pallas_call x1, Pallas kernels, gather_project(): pl.pallas_call(gather_kernel, out_shape=(jax.ShapeDtypeStruct((16 * rows,...  40.5 us
    pallas_call x1, Pallas kernels, project_scatter(): pl.pallas_call(functools.partial(scatter_kernel, rows), out_shape=(jax.Sh...  32.8 us
    ppermute x1, starting transfers between devices, from_behind(): return lax.ppermute(array, axis, pairs)  3.93 us
    unnamed x36, local copies, waits for them, and re-layouts  3.38 us
    dot_general x1, matrix products, decode_items(): jnp.einsum('nhp,shdp->nshd', features(queries), cache_own, precision=lax....  2.67 us
    dot_general x2, matrix products, local(): jnp.einsum('hij,jhd->ihd', weights, values[:finish], preferred_element_ty...  2.52 us
  transfers between devices with their start and end apart: 1, of which 0 were waited for; matrix products, arithmetic and copies ran while one was open for 7% of the time, Pallas kernels for 0%

profile of v5, /device:TPU:1, one launch (start us, length us, event | category | flops | bytes accessed | tf_op | source)
XLA Modules:
  0.0 107.6 jit_solution(8752439873483408724)
XLA Ops:
  0.7 1.1 %fusion.39 = f32[64]{0:T(128)S(1)} fusion(bf16[1,64,1792]{2,1,0:T(8,128)(2,1)} %param.14), kind=kLoop, calls=%fused_computation.55 | loop fusion | flops 344000 | bytes 229632 | tf_op jit(solution)/shard_map/reduce_sum | solution.py:415
  1.8 1.1 fusion.41
  2.9 3.9 %collective-permute-start = (bf16[2,1792]{1,0:T(2,128)(2,1)S(1)}, bf16[2,1792]{1,0:T(2,128)(2,1)S(1)}, u32[]{:S(2)}, u32[]{:S(2)}) collective-permute-start(bf16[2,1792]{1,0:T(2,128)(2,1)S(1)} %slice.97), channel_id=1, source_target_pairs={{0,32},{32,64},{64,96},{96,128},{128,160},{160,192},{192,224},{224... | collective-permute-start | bytes 21512 | tf_op jit(solution)/shard_map/ppermute | solution.py:410
  6.9 0.9 convert_reduce_fusion.1
  7.8 0.7 broadcast_add_fusion
  8.5 0.7 multiply_reduce_fusion.2
  9.2 0.9 slice_reduce_fusion.2
  11.8 0.8 select_reduce_fusion
  12.5 0.9 constant_dynamic-slice_fusion
  13.7 1.4 %copy.49 = bf16[1792,1,144]{2,0,1:T(8,128)(2,1)S(1)} copy(bf16[1792,1,144]{0,2,1:T(8,128)(2,1)} %param.20) | data formatting | bytes 1032192 | tf_op args[6]
  15.2 0.6 slice.88
  16.0 40.5 %gather_project.1 = (bf16[1024,144]{1,0:T(8,128)(2,1)S(1)}, f32[32,8,256]{2,1,0:T(8,128)S(1)}) custom-call(bf16[64,1792]{1,0:T(8,128)(2,1)S(1)} %fusion.43.own_ref, bf16[1792,144]{1,0:T(8,128)(2,1)S(1)} %bitcast.132, bf16[32,1792]{1,0:T(8,128)(2,1)S(1)} %bitcast.135, bf16[32,3584]{1,0:T(8,128)(2,1)S(1)} %bitcast.133, f32[1792]{0:T(1024)S(1)} %copy-done.3, ...), custom_call_target="tpu_custom_call" | custom-call | tf_op jit(solution)/shard_map/gather_project/pallas_call | solution.py:204
  56.6 1.2 %convert_reduce_fusion = s32[32,2]{1,0:T(8,128)} fusion(f32[32,8,256]{2,1,0:T(8,128)S(1)} %get-tuple-element.8), kind=kLoop, calls=%fused_computation.102 | loop fusion | flops 64 | bytes 512 | tf_op jit(solution)/shard_map/convert_element_type | solution.py:553
  58.2 0.3 fusion.52
  58.6 1.1 %fusion.47 = f32[1024,256]{0,1:T(8,128)S(1)} fusion(bf16[1024,1,144]{2,0,1:T(8,128)(2,1)S(1)} %bitcast.125, s32[256]{0:T(256)} %copy-done.10), kind=kOutput, calls=%fused_computation.67 | convolution fusion | flops 8392704 | bytes 1311744 | tf_op jit(solution)/shard_map/dot_general | solution.py:427
  59.7 0.9 multiply_bitcast_fusion
  60.9 2.7 %fusion = f32[64,16,112]{2,0,1:T(8,128)S(1)} fusion(f32[1,16,1,112,273]{3,2,4,1,0:T(1,128)} %param.23, f32[64,1,256]{2,0,1:T(8,128)S(1)} %fusion.17, f32[64,1,16]{2,0,1:T(8,128)S(1)} %get-tuple-element.29, f32[273]{0:T(512)S(1)} %pad.16.clone), kind=kOutput, calls=%fused_computation | convolution fusion | flops 187893888 | bytes 2486340 | tf_op jit(solution)/shard_map/nhp,shdp->nshd/dot_general | solution.py:451
  63.6 0.7 fusion.30
  64.3 0.2 multiply_reduce_fusion.1
  64.5 0.8 multiply_convert_fusion
  65.3 1.3 %fusion.5 = f32[1024,1,256]{0,2,1:T(8,128)} fusion(f32[1024,256]{0,1:T(8,128)S(1)} %fusion.52, bf16[1024,1,144]{2,0,1:T(8,128)(2,1)S(1)} %bitcast.127, s32[256]{0:T(256)S(1)} %and_select_fusion), kind=kOutput, calls=%fused_computation.9 | convolution fusion | flops 8916992 | bytes 2360320 | tf_op jit(solution)/shard_map/dot_general | solution.py:427
  66.6 1.8 %fusion.10 = f32[512,1,112]{2,0,1:T(8,128)} fusion(s32[512]{0:T(512)S(1)} %copy-done.12, pred[1024]{0:T(1024)(128)(4,1)S(1)} %copy-done.15, bf16[1024,1,144]{2,0,1:T(8,128)(2,1)S(1)} %bitcast.128), kind=kOutput, calls=%fused_computation.16 | convolution fusion | flops 138936320 | bytes 887808 | tf_op jit(solution)/shard_map/hij,jhd->ihd/dot_general | solution.py:534
  68.6 0.7 convolution_bitcast_fusion.1
  69.3 0.3 copy-done.4
  69.7 1.6 %multiply_reduce_fusion = (f32[1024]{0:T(1024)S(1)}, f32[1024,1,112]{2,0,1:T(8,128)S(1)}) fusion(f32[512,1,112]{2,0,1:T(8,128)S(1)} %copy-done.6, f32[512,1,112]{2,0,1:T(8,128)S(1)} %convolution_bitcast_fusion.1, f32[1024,1,256]{0,2,1:T(8,128)S(1)} %copy-done.4, f32[1024,1,16]{0,2,1:T(8,128)S(1)} %copy.51, f32[273]{0:T(512)S(1)} %pad.16.clone, ...), kind=kOutput, calls=%fused_computation.46 | convolution fusion | flops 188875776 | bytes 2159108 | tf_op jit(solution)/shard_map/ihp,hdp->ihd/dot_general | solution.py:512
  71.4 0.3 fusion.45.att_ref
  71.7 32.8 %project_scatter.1 = (bf16[64,1792]{1,0:T(8,128)(2,1)S(1)}, bf16[32,128]{1,0:T(8,128)(2,1)S(1)}) custom-call(bf16[1024,112]{1,0:T(8,128)(2,1)S(1)} %fusion.45.att_ref, bf16[112,1792]{1,0:T(8,128)(2,1)S(1)} %copy-done, f32[32,8,128]{2,1,0:T(8,128)S(1)} %pad_convert_fusion.served_ref, bf16[32,256]{1,0:T(8,128)(2,1)S(1)} %fusion.71.place_ref), custom_call_target="tpu_custom_call" | custom-call | tf_op jit(solution)/shard_map/project_scatter/pallas_call | solution.py:374
  104.5 0.6 broadcast_in_dim_reshape.2
  105.2 0.4 fusion.7
  105.7 0.4 fusion.15
  106.1 0.8 copy.60
  106.9 0.7 copy.91
  (73 shorter events, 2.1 us)
Async XLA Ops:
  0.6 14.5 %copy-start.7 = (bf16[1,32,2,1792]{3,2,1,0:T(2,128)(2,1)S(1)}, bf16[1,32,2,1792]{3,2,1,0:T(2,128)(2,1)}, u32[]{:S(2)}) copy-start(bf16[1,32,2,1792]{3,2,1,0:T(2,128)(2,1)} %param.17) | copy-start | bytes 688132
  0.6 15.1 %copy-start.11 = (bf16[1,2,1792]{2,1,0:T(2,128)(2,1)S(1)}, bf16[1,2,1792]{2,1,0:T(2,128)(2,1)}, u32[]{:S(2)}) copy-start(bf16[1,2,1792]{2,1,0:T(2,128)(2,1)} %param.15) | copy-start | bytes 21508
  2.9 12.9 %collective-permute-start = (bf16[2,1792]{1,0:T(2,128)(2,1)S(1)}, bf16[2,1792]{1,0:T(2,128)(2,1)S(1)}, u32[]{:S(2)}, u32[]{:S(2)}) collective-permute-start(bf16[2,1792]{1,0:T(2,128)(2,1)S(1)} %slice.97), channel_id=1, source_target_pairs={{0,32},{32,64},{64,96},{96,128},{128,160},{160,192},{192,224},{224... | collective-permute-start | bytes 21512 | tf_op jit(solution)/shard_map/ppermute | solution.py:410
  6.8 51.4 %copy-start.10 = (s32[256]{0:T(256)}, s32[256]{0:T(256)S(1)}, u32[]{:S(2)}) copy-start(s32[256]{0:T(256)S(1)} %and_select_fusion.1) | copy-start | bytes 3076
  13.5 1.7 %copy-start.14 = (pred[1024]{0:T(1024)(128)(4,1)}, pred[1024]{0:T(1024)(128)(4,1)S(1)}, u32[]{:S(2)}) copy-start(pred[1024]{0:T(1024)(128)(4,1)S(1)} %iota_compare_fusion.14) | copy-start | bytes 3076
  13.6 2.4 %copy-start.1 = (bf16[1,32,1792]{2,1,0:T(8,128)(2,1)S(1)}, bf16[1,32,1792]{2,1,0:T(8,128)(2,1)}, u32[]{:S(2)}) copy-start(bf16[1,32,1792]{2,1,0:T(8,128)(2,1)} %param.16) | copy-start | bytes 344068
  13.7 2.4 %copy-start.2 = (f32[3,1792]{1,0:T(4,128)S(1)}, f32[3,1792]{1,0:T(4,128)}, u32[]{:S(2)}) copy-start(f32[3,1792]{1,0:T(4,128)} %taps_ref.1) | copy-start | bytes 64516
  13.7 2.4 %copy-start.3 = (f32[1792]{0:T(1024)S(1)}, f32[1792]{0:T(1024)}, u32[]{:S(2)}) copy-start(f32[1792]{0:T(1024)} %gain_ref.1) | copy-start | bytes 21508
  15.1 41.4 %copy-start.9 = (s32[1024]{0:T(1024)}, s32[1024]{0:T(1024)S(1)}, u32[]{:S(2)}) copy-start(s32[1024]{0:T(1024)S(1)} %iota.59) | copy-start | bytes 12292
  57.9 2.7 %copy-start.8 = (s32[32,2]{1,0:T(8,128)S(1)}, s32[32,2]{1,0:T(8,128)}, u32[]{:S(2)}) copy-start(s32[32,2]{1,0:T(8,128)} %convert_reduce_fusion) | copy-start | bytes 772
  63.6 3.0 %copy-start.12 = (s32[512]{0:T(512)S(1)}, s32[512]{0:T(512)}, u32[]{:S(2)}) copy-start(s32[512]{0:T(512)} %slice.88) | copy-start | bytes 6148
  63.6 3.0 %copy-start.15 = (pred[1024]{0:T(1024)(128)(4,1)S(1)}, pred[1024]{0:T(1024)(128)(4,1)}, u32[]{:S(2)}) copy-start(pred[1024]{0:T(1024)(128)(4,1)} %copy-done.14) | copy-start | bytes 3076
  66.6 2.0 %slice-start = ((s32[1024]{0:T(1024)}), s32[512]{0:T(512)S(1)}, s32[]{:S(2)}) async-start(s32[1024]{0:T(1024)} %copy-done.9), calls=%async_computation | async-start | bytes 4096 | tf_op jit(solution)/shard_map/slice | solution.py:529
  66.6 2.0 %slice-start.1 = ((pred[1024]{0:T(1024)(128)(4,1)}), pred[512]{0:T(512)(128)(4,1)S(1)}, s32[]{:S(2)}) async-start(pred[1024]{0:T(1024)(128)(4,1)} %copy-done.14), calls=%async_computation.1 | async-start | bytes 1024 | tf_op jit(solution)/shard_map/slice | solution.py:529
  68.4 1.2 %copy-start.4 = (f32[1024,1,256]{0,2,1:T(8,128)S(1)}, f32[1024,1,256]{0,2,1:T(8,128)}, u32[]{:S(2)}) copy-start(f32[1024,1,256]{0,2,1:T(8,128)} %fusion.5) | copy-start | bytes 3145732
  68.6 1.1 %copy-start.6 = (f32[512,1,112]{2,0,1:T(8,128)S(1)}, f32[512,1,112]{2,0,1:T(8,128)}, u32[]{:S(2)}) copy-start(f32[512,1,112]{2,0,1:T(8,128)} %fusion.10) | copy-start | bytes 688132
  68.6 2.7 %copy-start.13 = (f32[112]{0:T(128)S(1)}, f32[112]{0:T(128)}, u32[]{:S(2)}) copy-start(f32[112]{0:T(128)} %param.21) | copy-start | bytes 1348
  69.7 2.0 %copy-start = (bf16[112,1792]{1,0:T(8,128)(2,1)S(1)}, bf16[112,1792]{1,0:T(8,128)(2,1)}, u32[]{:S(2)}) copy-start(bf16[112,1792]{1,0:T(8,128)(2,1)} %w_ref.1) | copy-start | bytes 1204228
  71.3 34.3 %copy-start.5 = (bf16[1024,1,1,1,1,1,16]{6,0,5,4,3,2,1:T(8,128)(2,1)S(1)}, bf16[1024,1,1,1,1,1,16]{6,0,5,4,3,2,1:T(8,128)(2,1)}, u32[]{:S(2)}) copy-start(bf16[1024,1,1,1,1,1,16]{6,0,5,4,3,2,1:T(8,128)(2,1)} %multiply_bitcast_fusion) | copy-start | bytes 98308
